TPU v7x, 32 devices: a whole 2x2x4 slice. The times are simulated.
32 devices in a mesh: seq: 8 (over z, x), tok: 4 (over y, core).
Axes of the slice: x: 2, y: 2, z: 4, core: 2. Of those that a mesh axis runs over, the one named last changes fastest.
Arguments:
- inputs: bfloat16 [16, 1536, 768], P('seq', 'tok'), may hold values from -6 to 6
- lengths: int32 [16], P('seq'), may hold values from 1024 to 1500, as said below
- matrices: float32 [7077888], P(('seq', 'tok')), may hold values from -2 to 2
- vectors: float32 [9216], P(('seq', 'tok')), may hold values from -2 to 2
- cotangent: bfloat16 [16, 1536, 768], P('seq', 'tok'), may hold values from -6 to 6
Outputs:
- outputs: bfloat16 [16, 1536, 768], P('seq', 'tok')
- grad_inputs: bfloat16 [16, 1536, 768], P('seq', 'tok')
- grad_matrices: float32 [7077888], P(('seq', 'tok'))
- grad_vectors: float32 [9216], P(('seq', 'tok'))
Inputs may be any that keep to these rules, and one draw needn't show every extreme that they name: `lengths`: the valid slots of a sequence are its first ones; both ends of the range occur in every draw.
All inputs are finite; a program needn't handle non-finite values.
Results may differ from a plain program's by a relative error of at most 0.015.
The roundings to bfloat16 on the way count: a program that leaves them out, or rounds other values in their place, can miss the bound.
Values may be sent and summed in bfloat16 or wider, within the bound.
A program may use at most 192 MiB of HBM per device.

v0:
```python
from functools import partial

import jax
import jax.numpy as jnp
from jax import lax
from jax.sharding import PartitionSpec as P

D = 768
HEADS = 12
HEAD = 64
FF = 3072


def layer_norm(token_rows, norm_gain, norm_shift):
    center = jnp.mean(token_rows, axis=-1, keepdims=True)
    centered = token_rows - center
    spread = jnp.mean(centered * centered, axis=-1, keepdims=True)
    return centered * lax.rsqrt(spread + 1e-05) * norm_gain + norm_shift


def split_matrices(flattened):
    square = D * D
    rectangle = D * FF
    w_query = flattened[0:square].reshape(D, D)
    w_key = flattened[square : 2 * square].reshape(D, D)
    w_value = flattened[2 * square : 3 * square].reshape(D, D)
    w_out = flattened[3 * square : 4 * square].reshape(D, D)
    w_up = flattened[4 * square : 4 * square + rectangle].reshape(D, FF)
    w_down = flattened[4 * square + rectangle : 4 * square + 2 * rectangle].reshape(FF, D)
    return (w_query, w_key, w_value, w_out, w_up, w_down)


def split_vectors(flattened):
    pieces = []
    for number in range(7):
        pieces.append(flattened[number * D : (number + 1) * D])
    pieces.append(flattened[7 * D : 7 * D + FF])
    pieces.append(flattened[7 * D + FF : 8 * D + FF])
    return tuple(pieces)


def matmul(left_operand, right_operand):
    return jnp.dot(left_operand, right_operand, preferred_element_type=jnp.float32)


def outer_sum(left_operand, right_operand):
    return lax.dot_general(
        left_operand, right_operand, (((0,), (0,)), ((), ())), preferred_element_type=jnp.float32
    )


def back_product(gradient, weight):
    return lax.dot_general(
        gradient, weight, (((1,), (1,)), ((), ())), preferred_element_type=jnp.float32
    )


def column_sum(gradient):
    return jnp.sum(gradient.astype(jnp.float32), axis=0)


def to_heads(frames, seq_count):
    return frames.reshape(seq_count, -1, HEADS, HEAD).transpose(2, 0, 1, 3)


def from_heads(per_head):
    head_count, seq_count, slot_count, head_size = per_head.shape
    return per_head.transpose(1, 2, 0, 3).reshape(seq_count, slot_count, head_count * head_size)


def head_scores(one_query, one_keys, key_valid):
    scores = jnp.einsum(
        "sqd,skd->sqk", one_query, one_keys, preferred_element_type=jnp.float32
    ) * HEAD ** (-0.5)
    return jnp.where(key_valid[:, None, :], scores, -1e30)


def local(inputs, lengths, matrices, vectors, cotangent):
    seq_count, local_slots, width = inputs.shape
    slot_total = local_slots * lax.axis_size("tok")
    matrices_low = matrices.astype(jnp.bfloat16)
    vectors_low = vectors.astype(jnp.bfloat16)
    gathered_mats, gathered_vecs = (
        lax.all_gather(matrices_low, ("seq", "tok"), axis=0, tiled=True),
        lax.all_gather(vectors_low, ("seq", "tok"), axis=0, tiled=True),
    )
    w_query, w_key, w_value, w_out, w_up, w_down = split_matrices(gathered_mats)
    (
        gain_one,
        first_norm_shift,
        bias_query,
        bias_value,
        bias_out,
        gain_two,
        shift_two,
        bias_up,
        bias_down,
    ) = split_vectors(gathered_vecs.astype(jnp.float32))
    token_rows = inputs.reshape(seq_count * local_slots, width).astype(jnp.float32)
    normed = layer_norm(token_rows, gain_one, first_norm_shift).astype(jnp.bfloat16)
    query = (matmul(normed, w_query) + bias_query).astype(jnp.bfloat16)
    keys_here = matmul(normed, w_key).astype(jnp.bfloat16)
    values_here = (matmul(normed, w_value) + bias_value).astype(jnp.bfloat16)
    key_valid = jnp.arange(slot_total, dtype=jnp.int32)[None, :] < lengths[:, None]
    all_keys, all_values = (
        lax.all_gather(keys_here.reshape(seq_count, local_slots, width), "tok", axis=1, tiled=True),
        lax.all_gather(
            values_here.reshape(seq_count, local_slots, width), "tok", axis=1, tiled=True
        ),
    )
    head_query = to_heads(query, seq_count)
    head_keys = to_heads(all_keys, seq_count)
    head_values = to_heads(all_values, seq_count)

    def attend(pieces):
        one_query, one_keys, one_values = pieces
        scores = head_scores(one_query, one_keys, key_valid)
        row_peak = jnp.max(scores, axis=-1, keepdims=True)
        raised = jnp.exp(scores - row_peak)
        overall_mass = jnp.sum(raised, axis=-1, keepdims=True)
        soft_low = (raised / overall_mass).astype(jnp.bfloat16)
        attended = jnp.einsum(
            "sqk,skd->sqd", soft_low, one_values, preferred_element_type=jnp.float32
        )
        return (attended.astype(jnp.bfloat16), row_peak + jnp.log(overall_mass))

    head_attended, log_mass = lax.map(attend, (head_query, head_keys, head_values))
    attended_rows = from_heads(head_attended).reshape(seq_count * local_slots, width)
    middle = token_rows + (matmul(attended_rows, w_out) + bias_out)
    normed_two = layer_norm(middle, gain_two, shift_two).astype(jnp.bfloat16)
    hidden = matmul(normed_two, w_up) + bias_up
    active = jax.nn.gelu(hidden, approximate=False).astype(jnp.bfloat16)
    result = middle + (matmul(active, w_down) + bias_down)
    outputs = result.astype(jnp.bfloat16).reshape(inputs.shape)
    back_mats, back_vecs = (
        lax.all_gather(matrices_low, ("seq", "tok"), axis=0, tiled=True),
        lax.all_gather(vectors_low, ("seq", "tok"), axis=0, tiled=True),
    )
    w_query, w_key, w_value, w_out, w_up, w_down = split_matrices(back_mats)
    (
        gain_one,
        first_norm_shift,
        bias_query,
        bias_value,
        bias_out,
        gain_two,
        shift_two,
        bias_up,
        bias_down,
    ) = split_vectors(back_vecs.astype(jnp.float32))
    grad_out = cotangent.reshape(seq_count * local_slots, width)
    grad_out_wide = grad_out.astype(jnp.float32)
    d_down = outer_sum(active, grad_out)
    down_bias_gradient = column_sum(grad_out)
    grad_active = back_product(grad_out, w_down)
    gelu_value, gelu_pull = jax.vjp(partial(jax.nn.gelu, approximate=False), hidden)
    grad_hidden = gelu_pull(grad_active)[0].astype(jnp.bfloat16)
    d_up = outer_sum(normed_two, grad_hidden)
    d_bias_up = column_sum(grad_hidden)
    grad_normed_two = back_product(grad_hidden, w_up)
    norm_value, norm_pull = jax.vjp(layer_norm, middle, gain_two, shift_two)
    grad_mid_norm, d_gain_two, d_shift_two = norm_pull(grad_normed_two)
    grad_middle = grad_out_wide + grad_mid_norm
    grad_branch = grad_middle.astype(jnp.bfloat16)
    d_out = outer_sum(attended_rows, grad_branch)
    d_bias_out = column_sum(grad_branch)
    grad_attended = back_product(grad_branch, w_out).astype(jnp.bfloat16)
    head_grads = to_heads(grad_attended, seq_count)

    def attend_back(pieces):
        one_query, one_keys, one_values, one_grad, one_mass = pieces
        scores = head_scores(one_query, one_keys, key_valid)
        soft_exact = jnp.exp(scores - one_mass)
        grad_values_part = jnp.einsum(
            "sqk,sqd->skd",
            soft_exact.astype(jnp.bfloat16),
            one_grad,
            preferred_element_type=jnp.float32,
        )
        grad_soft = jnp.einsum(
            "sqd,skd->sqk", one_grad, one_values, preferred_element_type=jnp.float32
        )
        inner_total = jnp.sum(grad_soft * soft_exact, axis=-1, keepdims=True)
        grad_scores = (soft_exact * (grad_soft - inner_total)).astype(jnp.bfloat16)
        grad_query_part = jnp.einsum(
            "sqk,skd->sqd", grad_scores, one_keys, preferred_element_type=jnp.float32
        ) * HEAD ** (-0.5)
        grad_keys_part = jnp.einsum(
            "sqk,sqd->skd", grad_scores, one_query, preferred_element_type=jnp.float32
        ) * HEAD ** (-0.5)
        return (grad_query_part.astype(jnp.bfloat16), grad_keys_part, grad_values_part)

    grad_query_heads, grad_keys_heads, grad_values_heads = lax.map(
        attend_back, (head_query, head_keys, head_values, head_grads, log_mass)
    )
    summed_keys, summed_values = (
        lax.psum_scatter(
            from_heads(grad_keys_heads).astype(jnp.bfloat16), "tok", scatter_dimension=1, tiled=True
        ).astype(jnp.float32),
        lax.psum_scatter(
            from_heads(grad_values_heads).astype(jnp.bfloat16),
            "tok",
            scatter_dimension=1,
            tiled=True,
        ).astype(jnp.float32),
    )
    grad_query = from_heads(grad_query_heads).reshape(seq_count * local_slots, width)
    grad_key = summed_keys.reshape(seq_count * local_slots, width).astype(jnp.bfloat16)
    grad_value = summed_values.reshape(seq_count * local_slots, width).astype(jnp.bfloat16)
    d_query = outer_sum(normed, grad_query)
    d_key = outer_sum(normed, grad_key)
    d_value = outer_sum(normed, grad_value)
    d_bias_query = column_sum(grad_query)
    d_bias_value = column_sum(grad_value)
    grad_normed = (
        back_product(grad_query, w_query)
        + back_product(grad_key, w_key)
        + back_product(grad_value, w_value)
    )
    first_value, leading_pullback = jax.vjp(layer_norm, token_rows, gain_one, first_norm_shift)
    grad_rows_norm, d_gain_one, d_shift_one = leading_pullback(grad_normed)
    grad_inputs = (grad_middle + grad_rows_norm).astype(jnp.bfloat16).reshape(inputs.shape)
    flat_matrix_grads = jnp.concatenate(
        [piece.reshape(-1) for piece in (d_query, d_key, d_value, d_out, d_up, d_down)]
    )
    flat_vector_grads = jnp.concatenate(
        [
            d_gain_one,
            d_shift_one,
            d_bias_query,
            d_bias_value,
            d_bias_out,
            d_gain_two,
            d_shift_two,
            d_bias_up,
            down_bias_gradient,
        ]
    )
    grad_matrices, grad_vectors = (
        lax.psum_scatter(flat_matrix_grads, ("seq", "tok"), scatter_dimension=0, tiled=True),
        lax.psum_scatter(flat_vector_grads, ("seq", "tok"), scatter_dimension=0, tiled=True),
    )
    return (outputs, grad_inputs, grad_matrices, grad_vectors)


def solution(mesh):
    in_specs = (
        P("seq", "tok", None),
        P("seq"),
        P(("seq", "tok")),
        P(("seq", "tok")),
        P("seq", "tok", None),
    )
    out_specs = (P("seq", "tok", None), P("seq", "tok", None), P(("seq", "tok")), P(("seq", "tok")))
    return jax.shard_map(local, mesh=mesh, in_specs=in_specs, out_specs=out_specs, check_vma=False)
```

profile of v0, /device:TPU:0, one launch (start us, length us, event | category | flops | bytes accessed | tf_op | source)
XLA Modules:
  0.0 1068.6 jit_solution(18270983424804290411)
XLA Ops:
  12.0 42.7 %all-reduce = bf16[9216]{0:T(1024)(128)(2,1)S(1)} all-reduce(bf16[9216]{0:T(1024)(128)(2,1)S(1)} %dynamic-update-slice), channel_id=1, replica_groups=mesh['seq'=8,'tok'=4] {'seq','tok'}, use_global_device_ids=true, to_apply=%add | all-reduce | flops 9216 | bytes 36864
  56.9 61.4 %all-gather.4.cloned.1.call-done = bf16[7077888]{0:T(1024)(128)(2,1)} async-done(((bf16[221184]{0:T(1024)(128)(2,1)}), bf16[7077888]{0:T(1024)(128)(2,1)}) %all-gather.4.cloned.1.call-update) | async-done | bytes 14155792 | tf_op jit(solution)/shard_map/all_gather | solution.py:84
  118.3 4.2 fusion.75
  136.7 4.0 add_convert_fusion.4
  143.4 8.3 fusion.74
  163.5 8.2 slice.129
  171.7 9.3 slice.132
  181.0 4.9 copy.57
  185.9 20.8 %all-gather.8.cloned.1.call-done = bf16[2,1536,768]{1,2,0:T(8,128)(2,1)} async-done(((bf16[2,384,768]{1,2,0:T(8,128)(2,1)}), bf16[2,1536,768]{1,2,0:T(8,128)(2,1)}) %all-gather.8.cloned.1.call-update) | async-done | bytes 4718608 | tf_op jit(solution)/shard_map/all_gather | solution.py:107
  206.7 5.0 copy.58
  211.9 71.4 %while.28 = (s32[]{:T(128)}, bf16[12,2,384,64]{2,3,1,0:T(8,128)(2,1)S(1)}, f32[12,2,384,1]{2,1,3,0:T(2,128)}, bf16[12,2,384,64]{2,3,1,0:T(8,128)(2,1)S(1)}, bf16...) while((s32[]{:T(128)}, ...), condition=%wide.region_5.6_spmd.clone, body=%wide.region_2.5_spmd.clone.sunk | while | flops 316197120 | bytes 15183977 | solution.py:127
  292.6 27.6 %convert_reduce_fusion = (f32[3072]{0:T(1024)}, bf16[768,3072]{1,0:T(8,128)(2,1)S(1)}, f32[768,3072]{1,0:T(8,128)}) fusion(f32[768,3072]{1,0:T(8,128)S(1)} %fusion.69, f32[3072]{0:T(1024)S(1)} %copy-done.35, bf16[768,768]{1,0:T(8,128)(2,1)S(1)} %bitcast.222, bf16[3072,768]{1,0:T(8,128)(2,1)S(1)} %bitcast.228), kind=kOutput, calls=%fused_computation.58 | convolution fusion | flops 3800822784 | bytes 29515776 | tf_op jit(solution)/shard_map/dot_general | solution.py:53
  320.2 4.8 multiply_reduce_fusion.1
  333.5 139.5 %while.29 = (s32[]{:T(128)}, bf16[12,2,384,64]{2,3,1,0:T(8,128)(2,1)S(1)}, bf16[12,2,1536,64]{2,3,0,1:T(8,128)(2,1)}, bf16[12,2,1536,64]{2,3,0,1:T(8,128)(2,1)},...) while((s32[]{:T(128)}, ...), condition=%wide.region_12.13_spmd.clone, body=%wide.region_10.12_spmd.clone.sunk | while | flops 765888768 | bytes 38854796 | solution.py:193
  473.0 12.7 %copy.78 = bf16[2,1536,768]{2,0,1:T(2,128)(2,1)} copy(bf16[2,1536,768]{1,2,0:T(8,128)(2,1)} %bitcast.229) | data formatting | bytes 9437184
  485.7 5.4 copy.108
  494.5 13.0 %copy.80 = bf16[2,1536,768]{2,0,1:T(2,128)(2,1)} copy(bf16[2,1536,768]{1,2,0:T(8,128)(2,1)} %bitcast.230) | data formatting | bytes 9437184
  507.5 5.6 copy.109
  518.1 7.0 convolution_bitcast_fusion.1
  525.1 11.1 %multiply_convert_fusion.1 = bf16[768,3072]{1,0:T(8,128)(2,1)} fusion(f32[768,3072]{1,0:T(8,128)} %get-tuple-element.235, f32[768,3072]{1,0:T(8,128)} %copy-done.10, f32[3072]{0:T(1024)} %slice.146), kind=kLoop, calls=%fused_computation.60 | loop fusion | flops 9437184 | bytes 23605248 | tf_op jit(solution)/shard_map/convert_element_type | solution.py:132
  536.3 4.2 fusion.80
  547.2 10.8 %copy.110 = f32[96,24,8,128]{3,1,2,0:T(8,128)} copy(f32[96,24,8,128]{3,2,1,0:T(8,128)} %convolution_bitcast_fusion.1) | data formatting | bytes 18874368
  558.0 8.6 fusion.82
  566.6 10.8 %reshape.313 = f32[2359296]{0:T(1024)} reshape(f32[3072,768]{1,0:T(8,128)} %fusion.82) | data formatting | bytes 18874368 | tf_op jit(solution)/shard_map/reshape | solution.py:224
  584.3 4.1 convolution_bitcast_fusion.3
  595.3 4.7 copy.81
  600.1 4.1 convolution_bitcast_fusion.2
  615.0 9.5 constant_dynamic-update-slice_fusion.3
  624.5 4.1 constant_dynamic-update-slice_fusion.2
  635.7 8.8 add_convert_fusion.2
  663.0 42.1 %all-reduce.2 = f32[9216]{0:T(1024)} all-reduce(f32[9216]{0:T(1024)} %constant_dynamic-update-slice_fusion.7), channel_id=5, replica_groups=mesh['seq'=8,'tok'=4] {'seq','tok'}, use_global_device_ids=true, to_apply=%region_27.28.clone | all-reduce | flops 9216 | bytes 73728
  709.9 349.4 %all-reduce.5.cloned.1.call-done = f32[7077888]{0:T(1024)} async-done(((f32[7077888]{0:T(1024)}), f32[7077888]{0:T(1024)}) %all-reduce.5.cloned.1.call-update) | async-done | bytes 28311568
  (389 shorter events, 335.9 us)
Async XLA Ops:
  7.2 111.1 %all-gather.4.cloned.1.call-start = ((), (), s32[]{:S(2)}) async-start(), calls=%async_computation.2 | async-start | bytes 14598144 | tf_op jit(solution)/shard_map/all_gather | solution.py:84
  9.3 171.7 %all-gather.6.cloned.1.call-start = ((), (), s32[]{:S(2)}) async-start(), calls=%async_computation.3 | async-start | bytes 5898240 | tf_op jit(solution)/shard_map/all_gather | solution.py:106
  10.3 112.1 %copy-start.29 = (f32[768]{0:T(1024)}, f32[768]{0:T(1024)S(1)}, u32[]{:S(2)}) copy-start(f32[768]{0:T(1024)S(1)} %div.51) | copy-start | bytes 9220
  11.4 45.4 %copy-start.31 = (f32[768]{0:T(1024)}, f32[768]{0:T(1024)S(1)}, u32[]{:S(2)}) copy-start(f32[768]{0:T(1024)S(1)} %rsqrt.25) | copy-start | bytes 9220
  55.4 67.1 %copy-start.27 = (f32[768]{0:T(1024)}, f32[768]{0:T(1024)S(1)}, u32[]{:S(2)}) copy-start(f32[768]{0:T(1024)S(1)} %get-tuple-element.256) | copy-start | bytes 9220
  55.4 232.2 %copy-start.25 = (f32[768]{0:T(1024)}, f32[768]{0:T(1024)S(1)}, u32[]{:S(2)}) copy-start(f32[768]{0:T(1024)S(1)} %get-tuple-element.252) | copy-start | bytes 9220
  132.0 4.7 copy-start.48
  132.0 74.7 %all-gather.8.cloned.1.call-start = ((), (), s32[]{:S(2)}) async-start(), calls=%async_computation.4 | async-start | bytes 5898240 | tf_op jit(solution)/shard_map/all_gather | solution.py:107
  143.1 437.5 %reduce-scatter.7.cloned.1.call-start = ((), (), s32[]{:S(2)}) async-start(), calls=%async_computation.5 | async-start | bytes 5898240
  206.7 5.2 copy-start.33
  287.1 5.4 slice-start.3
  292.6 27.6 %copy-start.10 = (f32[768,3072]{1,0:T(8,128)}, f32[768,3072]{1,0:T(8,128)S(1)}, u32[]{:S(2)}) copy-start(f32[768,3072]{1,0:T(8,128)S(1)} %fusion.69) | copy-start | bytes 28311556
  320.2 4.8 copy-start.16
  473.0 12.7 %copy-start.8 = (bf16[12,2,384,64]{2,3,1,0:T(8,128)(2,1)}, bf16[12,2,384,64]{2,3,1,0:T(8,128)(2,1)S(1)}, u32[]{:S(2)}) copy-start(bf16[12,2,384,64]{2,3,1,0:T(8,128)(2,1)S(1)} %get-tuple-element.98) | copy-start | bytes 3538948
  491.1 100.6 %reduce-scatter.9.cloned.1.call-start = ((), (), s32[]{:S(2)}) async-start(), calls=%async_computation.6 | async-start | bytes 5898240
  507.5 5.6 copy-start.9
  507.5 10.6 slice-start.7
  513.1 5.0 slice-start.8
  536.2 523.1 %all-reduce.5.cloned.1.call-start = ((), (), s32[]{:S(2)}) async-start(), calls=%async_computation.7 | async-start | bytes 56623104
  547.1 10.8 %copy-start.6 = (bf16[2,384,768]{2,1,0:T(8,128)(2,1)S(1)}, bf16[2,384,768]{2,1,0:T(8,128)(2,1)}, u32[]{:S(2)}) copy-start(bf16[2,384,768]{2,1,0:T(8,128)(2,1)} %param.13) | copy-start | bytes 3538948
  613.3 11.2 %slice-start = ((s8[9437184]{0:T(1024)(128)(4,1)}), s8[4194304]{0:T(1024)(128)(4,1)S(1)}, s32[]{:S(2)}) async-start(s8[9437184]{0:T(1024)(128)(4,1)} %bitcast.216), calls=%async_computation.8 | async-start | bytes 8388608
  615.0 9.5 slice-start.1
  615.0 9.5 slice-start.2
  635.7 8.8 copy-start.7
  648.9 6.2 copy-start.4
  648.9 6.0 copy-start.13
  649.0 7.5 copy-start.41
  649.0 8.8 copy-start.50
  649.0 10.1 copy-start.49
  649.0 11.3 %copy-start.44 = (f32[3072]{0:T(1024)S(1)}, f32[3072]{0:T(1024)}, u32[]{:S(2)}) copy-start(f32[3072]{0:T(1024)} %get-tuple-element.233) | copy-start | bytes 36868
  649.0 12.7 %copy-start.42 = (f32[768]{0:T(1024)S(1)}, f32[768]{0:T(1024)}, u32[]{:S(2)}) copy-start(f32[768]{0:T(1024)} %convert_reduce_fusion.2) | copy-start | bytes 9220
  649.0 57.3 %copy-start.3 = (f32[768,768]{1,0:T(8,128)S(1)}, f32[768,768]{1,0:T(8,128)}, u32[]{:S(2)}) copy-start(f32[768,768]{1,0:T(8,128)} %copy-done.2) | copy-start | bytes 7077892
  (34 other events, 70.4 us)
Sparse Core Ops, SparseCore 0:
  11.5 106.7 all-gather.3
  132.1 35.5 all-gather.5
  169.3 37.3 all-gather.7
  491.2 47.8 reduce-scatter.6
  541.6 47.8 reduce-scatter.8
  628.8 430.5 all-reduce.4
where the time goes:
time: 1080 us; the launch traced here: 1070 us
  waiting for transfers between devices  432 us (40%)
  matrix products  259 us (24%)
  local copies, waits for them, and re-layouts  217 us (20%)
  blocking collectives  84.8 us (8%)
  other arithmetic  59.6 us (6%)
  between operations  15 us (1%)
    unnamed x9, waiting for transfers between devices  350 us
    unnamed x151, local copies, waits for them, and re-layouts  112 us
    unnamed x2, blocking collectives  84.8 us
    all_gather x1, waiting for transfers between devices, local(): lax.all_gather(matrices_low, ('seq', 'tok'), axis=0, tiled=True)  61.4 us
    dot_general x24, matrix products, head_scores(): jnp.einsum('sqd,skd->sqk', one_query, one_keys, preferred_element_type=jn...  48.9 us
    dot_general x6, matrix products, back_product(): lax.dot_general(gradient, weight, (((1,), (1,)), ((), ())), preferred_ele...  39.9 us
    dot_general x6, matrix products, outer_sum(): lax.dot_general(left_operand, right_operand, (((0,), (0,)), ((), ())), pr...  30.7 us
    dot_general x12, matrix products, attend(): jnp.einsum('sqk,skd->sqd', soft_low, one_values, preferred_element_type=j...  27.4 us
  transfers between devices with their start and end apart: 6, of which 3 were waited for; matrix products, arithmetic and copies ran while one was open for 18% of the time, Pallas kernels for 0%

commit v1 on v0

v1 whole, which is shorter than its diff:
```python
from functools import partial

import jax
import jax.numpy as jnp
from jax import lax
from jax.experimental import pallas as pl
from jax.experimental.pallas import tpu as pltpu
from jax.sharding import PartitionSpec as P

D = 768
HEADS = 12
HEAD = 64
FF = 3072
PAIRS = HEADS // 2
LANES = 2 * HEAD
F32 = jnp.float32
BF16 = jnp.bfloat16
VMEM_LIMIT = 56 * 1024 * 1024


def layer_norm(token_rows, norm_gain, norm_shift):
    center = jnp.mean(token_rows, axis=-1, keepdims=True)
    centered = token_rows - center
    spread = jnp.mean(centered * centered, axis=-1, keepdims=True)
    return centered * lax.rsqrt(spread + 1e-05) * norm_gain + norm_shift


def matmul(left_operand, right_operand):
    return jnp.dot(left_operand, right_operand, preferred_element_type=F32)


def outer_sum(left_operand, right_operand):
    return lax.dot_general(
        left_operand, right_operand, (((0,), (0,)), ((), ())), preferred_element_type=F32
    )


def back_product(gradient, weight):
    return lax.dot_general(
        gradient, weight, (((1,), (1,)), ((), ())), preferred_element_type=F32
    )


def column_sum(gradient):
    return jnp.sum(gradient.astype(F32), axis=0)


def pair_columns(pair):
    return pl.ds(pl.multiple_of(pair * LANES, LANES), LANES)


def forward_pair(pair, q_ref, k_ref, v_ref, bias_ref, o_ref, l_ref, row_chunk):
    rows = q_ref.shape[0]
    keys = k_ref.shape[0]
    cols = pair_columns(pair)
    lane_k = lax.broadcasted_iota(jnp.int32, (keys, LANES), 1)
    lane_q = lax.broadcasted_iota(jnp.int32, (row_chunk, LANES), 1)
    lane_l = lax.broadcasted_iota(jnp.int32, (row_chunk, LANES), 1)
    key_pair = k_ref[:, cols]
    value_pair = v_ref[:, cols]
    bias = bias_ref[...]
    head_keys = []
    for half in range(2):
        own = lane_k // HEAD == half
        spare = lane_k == (1 - half) * HEAD
        head_keys.append(jnp.where(own, key_pair, jnp.where(spare, bias, jnp.zeros_like(bias))))
    for chunk in range(rows // row_chunk):
        part = pl.ds(chunk * row_chunk, row_chunk)
        query_pair = q_ref[part, cols]
        one = jnp.ones_like(query_pair)
        results = []
        masses = l_ref[part, :]
        for half in range(2):
            own_q = lane_q // HEAD == half
            query = jnp.where(own_q, query_pair, one)
            scores = lax.dot_general(
                query, head_keys[half], (((1,), (1,)), ((), ())), preferred_element_type=F32
            )
            peak = jnp.max(scores, axis=-1, keepdims=True)
            raised = jnp.exp(scores - peak)
            mass = jnp.sum(raised, axis=-1, keepdims=True)
            soft = (raised * (1.0 / mass)).astype(BF16)
            results.append(matmul(soft, value_pair))
            masses = jnp.where(lane_l == 2 * pair + half, peak + jnp.log(mass), masses)
        l_ref[part, :] = masses
        o_ref[part, cols] = jnp.where(lane_q // HEAD == 0, results[0], results[1]).astype(BF16)


def forward_kernel(row_chunk, q_ref, k_ref, v_ref, bias_ref, o_ref, lt_ref, l_ref):
    l_ref[...] = jnp.zeros_like(l_ref)

    def step(pair, carry):
        forward_pair(pair, q_ref, k_ref, v_ref, bias_ref, o_ref, l_ref, row_chunk)
        return carry

    lax.fori_loop(0, PAIRS, step, 0)
    lt_ref[...] = l_ref[...].T[: lt_ref.shape[0]]


def attend(query, keys, values, bias):
    rows = query.shape[0]
    vmem = pl.BlockSpec(memory_space=pltpu.VMEM)
    return pl.pallas_call(
        partial(forward_kernel, 256),
        out_shape=(
            jax.ShapeDtypeStruct((rows, D), BF16),
            jax.ShapeDtypeStruct((16, rows), F32),
        ),
        in_specs=[vmem] * 4,
        out_specs=(vmem, vmem),
        scratch_shapes=[pltpu.VMEM((rows, LANES), F32)],
        compiler_params=pltpu.CompilerParams(vmem_limit_bytes=VMEM_LIMIT),
        name="attend",
    )(query, keys, values, bias)


def backward_pair(
    pair, q_ref, k_ref, v_ref, bias_ref, g_ref, lt_ref, dt_ref, dq_ref, dk_ref, dv_ref, key_chunk
):
    rows = q_ref.shape[0]
    keys = k_ref.shape[0]
    cols = pair_columns(pair)
    lane_k = lax.broadcasted_iota(jnp.int32, (key_chunk, LANES), 1)
    lane_q = lax.broadcasted_iota(jnp.int32, (rows, LANES), 1)
    query_pair = q_ref[:, cols]
    grad_pair = g_ref[:, cols]
    one = jnp.ones_like(query_pair)
    query_heads = [jnp.where(lane_q // HEAD == half, query_pair, one) for half in range(2)]
    zero = jnp.zeros((key_chunk, LANES), BF16)
    grad_query = [jnp.zeros((rows, LANES), F32) for _ in range(2)]
    for chunk in range(keys // key_chunk):
        part = pl.ds(chunk * key_chunk, key_chunk)
        key_pair = k_ref[part, cols]
        value_pair = v_ref[part, cols]
        bias = bias_ref[part, :]
        grad_key = []
        grad_value = []
        for half in range(2):
            own = lane_k // HEAD == half
            spare = lane_k == (1 - half) * HEAD
            head_key = jnp.where(own, key_pair, jnp.where(spare, bias, jnp.zeros_like(bias)))
            head_value = jnp.where(own, value_pair, zero)
            scores = back_product(head_key, query_heads[half])
            mass = lt_ref[pl.ds(2 * pair + half, 1), :]
            inner = dt_ref[pl.ds(2 * pair + half, 1), :]
            soft = jnp.exp(scores - mass)
            grad_soft = back_product(head_value, grad_pair)
            grad_scores = (soft * (grad_soft - inner)).astype(BF16)
            grad_value.append(matmul(soft.astype(BF16), grad_pair))
            grad_key.append(matmul(grad_scores, query_pair))
            grad_query[half] = grad_query[half] + outer_sum(grad_scores, key_pair)
        first = lane_k // HEAD == 0
        dk_ref[part, cols] = jnp.where(first, grad_key[0], grad_key[1]).astype(BF16)
        dv_ref[part, cols] = jnp.where(first, grad_value[0], grad_value[1]).astype(BF16)
    merged = jnp.where(lane_q // HEAD == 0, grad_query[0], grad_query[1])
    dq_ref[:, cols] = (merged * HEAD ** (-0.5)).astype(BF16)


def backward_kernel(key_chunk, *refs):
    def step(pair, carry):
        backward_pair(pair, *refs, key_chunk)
        return carry

    lax.fori_loop(0, PAIRS, step, 0)


def attend_back(query, keys, values, bias, grad, lt, dt):
    vmem = pl.BlockSpec(memory_space=pltpu.VMEM)
    return pl.pallas_call(
        partial(backward_kernel, 256),
        out_shape=(
            jax.ShapeDtypeStruct(query.shape, BF16),
            jax.ShapeDtypeStruct(keys.shape, BF16),
            jax.ShapeDtypeStruct(keys.shape, BF16),
        ),
        in_specs=[vmem] * 7,
        out_specs=(vmem,) * 3,
        compiler_params=pltpu.CompilerParams(vmem_limit_bytes=VMEM_LIMIT),
        name="attend_back",
    )(query, keys, values, bias, grad, lt, dt)


def split_matrices(rows):
    w_up = rows[4 * D : 4 * D + FF].reshape(D, FF)
    w_down = rows[4 * D + FF : 4 * D + 2 * FF]
    return (rows[:D], rows[D : 2 * D], rows[2 * D : 3 * D], rows[3 * D : 4 * D], w_up, w_down)


def split_vectors(flattened):
    pieces = []
    for number in range(7):
        pieces.append(flattened[number * D : (number + 1) * D])
    pieces.append(flattened[7 * D : 7 * D + FF])
    pieces.append(flattened[7 * D + FF : 8 * D + FF])
    return tuple(pieces)


def local(inputs, lengths, matrices, vectors, cotangent):
    seq_count, local_slots, width = inputs.shape
    tok_size = lax.axis_size("tok")
    tok = lax.axis_index("tok")
    half = tok // 2
    devices = tok_size * lax.axis_size("seq")
    rows = seq_count * local_slots
    across = [(i, (i + 2) % 4) for i in range(4)]
    partner = [(i, i + 1 - 2 * (i % 2)) for i in range(4)]

    def pick(array, index):
        return lax.dynamic_index_in_dim(array, index, 0, keepdims=False)

    def to_sequence(array):
        other = lax.ppermute(pick(array, 1 - half), "tok", across)
        return jnp.concatenate([pick(array, half), other], axis=0)

    def from_sequence(array):
        other = lax.ppermute(array[local_slots:], "tok", across)
        kept = array[:local_slots]
        return jnp.where(half == 0, jnp.stack([kept, other]), jnp.stack([other, kept]))

    shard_rows = matrices.shape[0] // width
    low_rows = matrices.reshape(shard_rows, width).astype(BF16)
    gathered = lax.all_gather(low_rows, ("seq", "tok"), axis=0, tiled=True)
    w_query, w_key, w_value, w_out, w_up, w_down = split_matrices(gathered)
    vec_count = vectors.shape[0]
    vec_rows = 8
    vec_pad = vec_rows * 128 - vec_count
    vec_low = jnp.pad(vectors, (0, vec_pad)).astype(BF16).reshape(vec_rows, 128)
    vecs = lax.all_gather(vec_low, ("seq", "tok"), axis=0, tiled=True)
    vecs = vecs.reshape(devices, vec_rows * 128)[:, :vec_count].reshape(-1)
    (
        gain_one,
        first_norm_shift,
        bias_query,
        bias_value,
        bias_out,
        gain_two,
        shift_two,
        bias_up,
        bias_down,
    ) = split_vectors(vecs.astype(F32))

    token_rows = to_sequence(inputs).astype(F32)
    grad_out = to_sequence(cotangent)
    length = pick(lengths, half)
    slot = jnp.arange(local_slots, dtype=jnp.int32)
    places = jnp.concatenate([block * local_slots + slot for block in (tok, tok ^ 2, tok ^ 1, tok ^ 3)])
    bias = jnp.where(places < length, 0.0, -1e30).astype(BF16)[:, None]
    bias = jnp.broadcast_to(bias, (bias.shape[0], LANES))

    normed = layer_norm(token_rows, gain_one, first_norm_shift).astype(BF16)
    query = (matmul(normed, w_query) + bias_query).astype(BF16)
    scaled = query * jnp.asarray(HEAD ** (-0.5), BF16)
    keys_here = matmul(normed, w_key).astype(BF16)
    values_here = (matmul(normed, w_value) + bias_value).astype(BF16)
    keys = jnp.concatenate([keys_here, lax.ppermute(keys_here, "tok", partner)], axis=0)
    values = jnp.concatenate([values_here, lax.ppermute(values_here, "tok", partner)], axis=0)
    attended, lt = attend(scaled, keys, values, bias)
    middle = token_rows + (matmul(attended, w_out) + bias_out)
    normed_two = layer_norm(middle, gain_two, shift_two).astype(BF16)
    hidden = matmul(normed_two, w_up) + bias_up
    active = jax.nn.gelu(hidden, approximate=False).astype(BF16)
    result = middle + (matmul(active, w_down) + bias_down)
    outputs = from_sequence(result.astype(BF16))

    grad_out_wide = grad_out.astype(F32)
    d_down = outer_sum(active, grad_out)
    down_bias_gradient = column_sum(grad_out)
    grad_active = back_product(grad_out, w_down)
    gelu_value, gelu_pull = jax.vjp(partial(jax.nn.gelu, approximate=False), hidden)
    grad_hidden = gelu_pull(grad_active)[0].astype(BF16)
    d_up = outer_sum(normed_two, grad_hidden)
    d_bias_up = column_sum(grad_hidden)
    grad_normed_two = back_product(grad_hidden, w_up)
    norm_value, norm_pull = jax.vjp(layer_norm, middle, gain_two, shift_two)
    grad_mid_norm, d_gain_two, d_shift_two = norm_pull(grad_normed_two)
    grad_middle = grad_out_wide + grad_mid_norm
    grad_branch = grad_middle.astype(BF16)
    d_out = outer_sum(attended, grad_branch)
    d_bias_out = column_sum(grad_branch)
    grad_attended = back_product(grad_branch, w_out).astype(BF16)
    inner = (grad_attended.astype(F32) * attended.astype(F32)).reshape(rows, HEADS, HEAD).sum(-1)
    inner = jnp.pad(inner.T, ((0, 16 - HEADS), (0, 0)))
    grad_query, grad_keys, grad_values = attend_back(
        scaled, keys, values, bias, grad_attended, lt, inner
    )

    def pair_sum(array):
        other = lax.ppermute(array[rows:], "tok", partner)
        return (array[:rows].astype(F32) + other.astype(F32)).astype(BF16)

    grad_key = pair_sum(grad_keys)
    grad_value = pair_sum(grad_values)
    d_query = outer_sum(normed, grad_query)
    d_key = outer_sum(normed, grad_key)
    d_value = outer_sum(normed, grad_value)
    d_bias_query = column_sum(grad_query)
    d_bias_value = column_sum(grad_value)
    grad_normed = (
        back_product(grad_query, w_query)
        + back_product(grad_key, w_key)
        + back_product(grad_value, w_value)
    )
    first_value, leading_pullback = jax.vjp(layer_norm, token_rows, gain_one, first_norm_shift)
    grad_rows_norm, d_gain_one, d_shift_one = leading_pullback(grad_normed)
    grad_inputs = from_sequence((grad_middle + grad_rows_norm).astype(BF16))
    matrix_rows = jnp.concatenate(
        [
            piece.astype(BF16).reshape(-1, width)
            for piece in (d_query, d_key, d_value, d_out, d_up, d_down)
        ]
    )
    flat_vector_grads = jnp.concatenate(
        [
            d_gain_one,
            d_shift_one,
            d_bias_query,
            d_bias_value,
            d_bias_out,
            d_gain_two,
            d_shift_two,
            d_bias_up,
            down_bias_gradient,
        ]
    )
    vector_rows = jnp.pad(flat_vector_grads.reshape(devices, vec_count), ((0, 0), (0, vec_pad)))
    grad_rows = lax.psum_scatter(
        matrix_rows, ("seq", "tok"), scatter_dimension=0, tiled=True
    )
    grad_vec_rows = lax.psum_scatter(
        vector_rows.reshape(devices * vec_rows, 128), ("seq", "tok"), scatter_dimension=0, tiled=True
    )
    grad_matrices = grad_rows.astype(F32).reshape(-1)
    grad_vectors = grad_vec_rows.reshape(-1)[:vec_count]
    return (outputs, grad_inputs, grad_matrices, grad_vectors)


def solution(mesh):
    in_specs = (
        P("seq", "tok", None),
        P("seq"),
        P(("seq", "tok")),
        P(("seq", "tok")),
        P("seq", "tok", None),
    )
    out_specs = (P("seq", "tok", None), P("seq", "tok", None), P(("seq", "tok")), P(("seq", "tok")))
    return jax.shard_map(local, mesh=mesh, in_specs=in_specs, out_specs=out_specs, check_vma=False)
```

time: 1080 us -> 667 us (0.62)
  matrix products: 259 us -> 106 us
  local copies, waits for them, and re-layouts: 217 us -> 72.9 us
  waiting for transfers between devices: 432 us -> 304 us
  Pallas kernels: 0 us -> 80.4 us
  other arithmetic: 59.6 us -> 22.8 us
  blocking collectives: 84.8 us -> 51.6 us
    unnamed x9 -> x4, waiting for transfers between devices: 350 us -> 74.8 us
    reduce_scatter x0 -> x1, waiting for transfers between devices: none -> 165 us  [local(): lax.psum_scatter(matrix_rows, ('seq', 'tok'), scatter_dimension=0, tiled=...]
    dot_general x90 -> x6, matrix products: 189 us -> 48.5 us  [matmul(): return jnp.dot(left_operand, right_operand, preferred_element_type=F32)]
    unnamed x151 -> x119, local copies, waits for them, and re-layouts: 112 us -> 17.4 us
    unnamed x2 -> x0, blocking collectives: 84.8 us -> none
    pallas_call x0 -> x2, Pallas kernels: none -> 80.4 us  [the longest x1 45.3 us: attend_back(): pl.pallas_call(partial(backward_kernel, 256), out_shape=(jax.ShapeDtypeSt...]
    all_gather x0 -> x1, blocking collectives: none -> 51.6 us  [local(): vecs = lax.all_gather(vec_low, ('seq', 'tok'), axis=0, tiled=True)]
    all_gather x3 -> x1, waiting for transfers between devices: 82.1 us -> 50.4 us  [local(): gathered = lax.all_gather(low_rows, ('seq', 'tok'), axis=0, tiled=True)]
  transfers between devices with their start and end apart: 6 -> 11, of which waited for: 3 -> 4; matrix products, arithmetic and copies ran while one was open for 18% -> 19% of each run, Pallas kernels for 0% -> 5%
where the time goes in v1:
time: 667 us; the launch traced here: 660 us
  waiting for transfers between devices  304 us (46%)
  matrix products  106 us (16%)
  Pallas kernels  80.4 us (12%)
  local copies, waits for them, and re-layouts  72.9 us (11%)
  blocking collectives  51.6 us (8%)
  other arithmetic  22.8 us (3%)
  between operations  14.6 us (2%)
  starting transfers between devices  7.8 us (1%)
    reduce_scatter x1, waiting for transfers between devices, local(): lax.psum_scatter(matrix_rows, ('seq', 'tok'), scatter_dimension=0, tiled=...  165 us
    unnamed x4, waiting for transfers between devices  74.8 us
    all_gather x1, blocking collectives, local(): vecs = lax.all_gather(vec_low, ('seq', 'tok'), axis=0, tiled=True)  51.6 us
    all_gather x1, waiting for transfers between devices, local(): gathered = lax.all_gather(low_rows, ('seq', 'tok'), axis=0, tiled=True)  50.4 us
    dot_general x6, matrix products, matmul(): return jnp.dot(left_operand, right_operand, preferred_element_type=F32)  48.5 us
    pallas_call x1, Pallas kernels, attend_back(): pl.pallas_call(partial(backward_kernel, 256), out_shape=(jax.ShapeDtypeSt...  45.3 us
    pallas_call x1, Pallas kernels, attend(): pl.pallas_call(partial(forward_kernel, 256), out_shape=(jax.ShapeDtypeStr...  35.1 us
    dot_general x6, matrix products, back_product(): lax.dot_general(gradient, weight, (((1,), (1,)), ((), ())), preferred_ele...  31.5 us
  transfers between devices with their start and end apart: 11, of which 4 were waited for; matrix products, arithmetic and copies ran while one was open for 19% of the time, Pallas kernels for 5%

profile of v1, /device:TPU:0, one launch (start us, length us, event | category | flops | bytes accessed | tf_op | source)
XLA Modules:
  0.0 660.0 jit_solution(9229653347778063394)
XLA Ops:
  11.8 3.0 collective-permute-start
  14.8 51.6 %all_gather.6 = bf16[256,128]{1,0:T(8,128)(2,1)S(1)} all-gather(bf16[8,128]{1,0:T(8,128)(2,1)S(1)} %pad_bitcast_fusion), channel_id=1, replica_groups=mesh['seq'=8,'tok'=4] {'seq','tok'}, dimensions={0}, use_global_device_ids=true | all-gather | bytes 67584 | tf_op jit(solution)/shard_map/all_gather | solution.py:228
  69.5 50.4 %all-gather.2.cloned.1.call-done = bf16[9216,768]{1,0:T(8,128)(2,1)} async-done(((bf16[288,768]{1,0:T(8,128)(2,1)}), bf16[9216,768]{1,0:T(8,128)(2,1)}) %all-gather.2.cloned.1.call-update) | async-done | bytes 14155792 | tf_op jit(solution)/shard_map/all_gather | solution.py:222
  120.0 3.6 convolution_convert_fusion.7
  123.9 2.6 add_convert_fusion.6
  133.0 4.9 slice.112
  137.9 8.6 %reshape.141 = bf16[768,3072]{1,0:T(8,128)(2,1)} reshape(bf16[3072,768]{1,0:T(8,128)(2,1)} %slice.112) | data formatting | bytes 9437184 | tf_op jit(solution)/shard_map/reshape | solution.py:184
  146.5 3.6 fusion.31.q_ref.refs_0_
  150.2 3.2 pad_maximum_fusion.k_ref.refs_1_
  153.3 2.9 pad_maximum_fusion.1.v_ref.refs_2_
  157.2 35.1 %attend.1 = (bf16[768,768]{1,0:T(8,128)(2,1)}, f32[16,768]{1,0:T(8,128)}) custom-call(bf16[768,768]{1,0:T(8,128)(2,1)} %fusion.31.q_ref.refs_0_, bf16[1536,768]{1,0:T(8,128)(2,1)} %pad_maximum_fusion.k_ref.refs_1_, bf16[1536,768]{1,0:T(8,128)(2,1)} %pad_maximum_fusion.1.v_ref.refs_2_, bf16[1536,128]{1,0:T(8,128)(2,1)} %broadcast_in_dim.20.bias_ref.refs_3_), custom_call_target="tpu_custom_call" | custom-call | tf_op jit(solution)/shard_map/attend/pallas_call | solution.py:103
  192.3 3.0 fusion.57
  196.0 27.9 %multiply_convert_fusion = (bf16[768,3072]{1,0:T(8,128)(2,1)}, f32[768,3072]{1,0:T(8,128)}, f32[768,3072]{1,0:T(8,128)}) fusion(f32[3072]{0:T(1024)S(1)} %copy-done.33, bf16[768,3072]{1,0:T(8,128)(2,1)S(1)} %bitcast.49, f32[768,768]{0,1:T(8,128)S(1)} %get-tuple-element.57, f32[768]{0:T(1024)S(1)} %copy-done.39, f32[768]{0:T(1024)S(1)} %copy-done.24, ...), kind=kOutput, calls=%fused_computation.4 | convolution fusion | flops 3782541312 | bytes 30695424 | tf_op jit(solution)/shard_map/dot_general | solution.py:29
  223.9 12.5 %convert_reduce_fusion = (f32[3072]{0:T(1024)}, bf16[768,3072]{1,0:T(8,128)(2,1)S(1)}) fusion(f32[768,3072]{1,0:T(8,128)} %get-tuple-element.37, bf16[9216,768]{1,0:T(8,128)(2,1)} %all-gather.2.cloned.1.call-done, bf16[384,768]{0,1:T(8,128)(2,1)} %collective-permute-done.4, bf16[384,768]{0,1:T(8,128)(2,1)S(1)} %bitcast.44, ...), kind=kOutput, calls=%fused_computation.2 | convolution fusion | flops 3666342912 | bytes 29515776 | tf_op jit(solution)/shard_map/dot_general | solution.py:39
  236.4 5.9 fusion.58
  242.3 3.1 copy.41
  245.4 3.1 multiply_reduce_fusion
  252.2 4.6 convert_multiply_fusion
  256.8 3.1 copy.43
  263.8 45.3 %attend_back.1 = (bf16[768,768]{1,0:T(8,128)(2,1)}, bf16[1536,768]{1,0:T(8,128)(2,1)}, bf16[1536,768]{1,0:T(8,128)(2,1)}) custom-call(bf16[768,768]{1,0:T(8,128)(2,1)} %fusion.31.q_ref.refs_0_, bf16[1536,768]{1,0:T(8,128)(2,1)} %pad_maximum_fusion.k_ref.refs_1_, bf16[1536,768]{1,0:T(8,128)(2,1)} %pad_maximum_fusion.1.v_ref.refs_2_, ...), custom_call_target="tpu_custom_call" | custom-call | tf_op jit(solution)/shard_map/attend_back/pallas_call | solution.py:169
  311.5 8.0 %convolution_convert_fusion.1 = bf16[768,3072]{1,0:T(8,128)(2,1)} fusion(bf16[768,3072]{1,0:T(8,128)(2,1)} %copy-done.47, f32[768,768]{0,1:T(8,128)S(1)} %get-tuple-element.57, f32[768]{0:T(1024)S(1)} %copy-done.40, f32[768]{0:T(1024)S(1)} %copy-done.26, f32[768]{0:T(1024)S(1)} %copy-done.29, f32[768]{0:T(1024)S(1)} %broadcast_multiply_fusion), kind=kOutput, calls=%fused_computation.20 | convolution fusion | flops 3629187072 | bytes 11808768 | tf_op jit(solution)/shard_map/dot_general | solution.py:33
  319.5 8.7 %reshape.143 = bf16[3072,768]{1,0:T(8,128)(2,1)} reshape(bf16[768,3072]{1,0:T(8,128)(2,1)} %convolution_convert_fusion.1) | data formatting | bytes 9437184 | tf_op jit(solution)/shard_map/reshape | solution.py:308
  335.2 2.9 fusion.36
  338.1 3.1 fusion.52
  353.1 3.3 convert_reduce_fusion.2
  362.3 4.2 fusion.28
  371.3 2.5 constant_dynamic-update-slice_fusion
  373.9 7.0 %fusion.6 = bf16[9216,768]{1,0:T(8,128)(2,1)} fusion(bf16[9216,768]{1,0:T(8,128)(2,1)} %constant_dynamic-update-slice_fusion, bf16[768,3072]{1,0:T(8,128)(2,1)S(1)} %bitcast.56, bf16[384,768]{0,1:T(8,128)(2,1)} %collective-permute-done.4, bf16[384,768]{0,1:T(8,128)(2,1)S(1)} %bitcast.47), kind=kOutput, calls=%fused_computation.19 | convolution fusion | flops 3628597248 | bytes 10616832 | tf_op jit(solution)/shard_map/dot_general | solution.py:33
  381.5 7.7 %add_convert_fusion.4 = bf16[768,768]{0,1:T(8,128)(2,1)S(1)} fusion(f32[768,768]{0,1:T(8,128)S(1)} %get-tuple-element.57, bf16[768,3072]{1,0:T(8,128)(2,1)} %get-tuple-element.36, bf16[9216,768]{1,0:T(8,128)(2,1)} %all-gather.2.cloned.1.call-done, f32[768]{0:T(1024)S(1)} %copy-done.34), kind=kOutput, calls=%fused_computation.55 | convolution fusion | flops 3625648128 | bytes 12979200 | tf_op jit(solution)/shard_map/dot_general | solution.py:29
  393.1 13.6 %collective-permute-done.3 = bf16[384,768]{0,1:T(8,128)(2,1)S(1)} collective-permute-done((bf16[384,768]{0,1:T(8,128)(2,1)}, bf16[384,768]{0,1:T(8,128)(2,1)S(1)}, u32[]{:S(2)}, u32[]{:S(2)}) %collective-permute-start.3) | collective-permute-done | bytes 589856 | tf_op jit(solution)/shard_map/ppermute | solution.py:216
  408.4 74.7 %all-reduce.6.cloned.1.call-done = f32[256,128]{1,0:T(8,128)} async-done(((f32[256,128]{1,0:T(8,128)}), f32[256,128]{1,0:T(8,128)}) %all-reduce.6.cloned.1.call-update) | async-done | bytes 131088
  486.1 164.8 %reduce-scatter.2.cloned.1.call-done = bf16[288,768]{1,0:T(8,128)(2,1)} async-done(((bf16[9216,768]{1,0:T(8,128)(2,1)}), bf16[288,768]{1,0:T(8,128)(2,1)}) %reduce-scatter.2.cloned.1.call-update) | async-done | bytes 442384 | tf_op jit(solution)/shard_map/reduce_scatter | solution.py:326
  (196 shorter events, 66.7 us)
Async XLA Ops:
  7.2 112.8 %all-gather.2.cloned.1.call-start = ((), (), s32[]{:S(2)}) async-start(), calls=%async_computation.1 | async-start | bytes 14598144 | tf_op jit(solution)/shard_map/all_gather | solution.py:222
  9.6 473.6 %all-reduce.6.cloned.1.call-start = ((), (), s32[]{:S(2)}) async-start(), calls=%async_computation.3 | async-start | bytes 262144
  9.7 5.1 copy-start.45
  11.8 57.2 %collective-permute-start = (bf16[384,768]{0,1:T(8,128)(2,1)S(1)}, bf16[384,768]{0,1:T(8,128)(2,1)S(1)}, u32[]{:S(2)}, u32[]{:S(2)}) collective-permute-start(bf16[384,768]{0,1:T(8,128)(2,1)S(1)} %bitcast.53), channel_id=1, source_target_pairs={{0,2},{1,3},{2,0},{3,1},{4,6},{5,7},{6,4},{7,5},{8,10},{9,11},{10,... | collective-permute-start | bytes 1769480 | tf_op jit(solution)/shard_map/ppermute | solution.py:212
  68.9 54.7 %copy-start.35 = (f32[768]{0:T(1024)}, f32[768]{0:T(1024)S(1)}, u32[]{:S(2)}) copy-start(f32[768]{0:T(1024)S(1)} %get-tuple-element.54) | copy-start | bytes 9220
  69.5 54.1 %copy-start.20 = (f32[768]{0:T(1024)}, f32[768]{0:T(1024)S(1)}, u32[]{:S(2)}) copy-start(f32[768]{0:T(1024)S(1)} %fusion.22) | copy-start | bytes 9220
  123.6 26.6 %collective-permute-start.1 = (bf16[768,768]{1,0:T(8,128)(2,1)}, bf16[768,768]{1,0:T(8,128)(2,1)}, u32[]{:S(2)}, u32[]{:S(2)}) collective-permute-start(bf16[768,768]{1,0:T(8,128)(2,1)} %convolution_convert_fusion.7), channel_id=1, source_target_pairs={{0,1},{1,0},{2,3},{3,2},{4,5},{5,4},{6,7},{7,6},{8,9},{9,8},{10,11... | collective-permute-start | bytes 3538952 | tf_op jit(solution)/shard_map/ppermute | solution.py:255
  123.9 6.8 %copy-start.46 = (s32[2]{0:T(128)S(1)}, s32[2]{0:T(128)}, u32[]{:S(2)}) copy-start(s32[2]{0:T(128)} %param.6) | copy-start | bytes 28
  126.5 26.8 %collective-permute-start.2 = (bf16[768,768]{1,0:T(8,128)(2,1)S(1)}, bf16[768,768]{1,0:T(8,128)(2,1)}, u32[]{:S(2)}, u32[]{:S(2)}) collective-permute-start(bf16[768,768]{1,0:T(8,128)(2,1)S(1)} %add_convert_fusion.6), channel_id=1, source_target_pairs={{0,1},{1,0},{2,3},{3,2},{4,5},{5,4},{6,7},{7,6},{8,9},{9,8},{10,11... | collective-permute-start | bytes 3538952 | tf_op jit(solution)/shard_map/ppermute | solution.py:256
  127.9 96.0 %collective-permute-start.4 = (bf16[384,768]{0,1:T(8,128)(2,1)}, bf16[384,768]{0,1:T(8,128)(2,1)}, u32[]{:S(2)}, u32[]{:S(2)}) collective-permute-start(bf16[384,768]{0,1:T(8,128)(2,1)} %bitcast.52), channel_id=1, source_target_pairs={{0,2},{1,3},{2,0},{3,1},{4,6},{5,7},{6,4},{7,5},{8,10},{9,11},{10,... | collective-permute-start | bytes 1769480 | tf_op jit(solution)/shard_map/ppermute | solution.py:212
  137.9 8.6 %copy-start.36 = (f32[768]{0:T(1024)S(1)}, f32[768]{0:T(1024)}, u32[]{:S(2)}) copy-start(f32[768]{0:T(1024)} %copy-done.35) | copy-start | bytes 9220
  137.9 8.6 %copy-start.42 = (f32[768]{0:T(1024)S(1)}, f32[768]{0:T(1024)}, u32[]{:S(2)}) copy-start(f32[768]{0:T(1024)} %get-tuple-element.53) | copy-start | bytes 9220
  157.2 35.1 %copy-start.41 = (f32[768]{0:T(1024)S(1)}, f32[768]{0:T(1024)}, u32[]{:S(2)}) copy-start(f32[768]{0:T(1024)} %get-tuple-element.51) | copy-start | bytes 9220
  195.6 28.3 %copy-start.22 = (f32[768]{0:T(1024)}, f32[768]{0:T(1024)S(1)}, u32[]{:S(2)}) copy-start(f32[768]{0:T(1024)S(1)} %multiply_reduce_fusion.2) | copy-start | bytes 9220
  195.7 28.2 %copy-start.27 = (f32[768]{0:T(1024)}, f32[768]{0:T(1024)S(1)}, u32[]{:S(2)}) copy-start(f32[768]{0:T(1024)S(1)} %fusion.44) | copy-start | bytes 9220
  196.0 27.9 %copy-start.3 = (bf16[1,384,768]{1,2,0:T(8,128)(2,1)S(1)}, bf16[1,384,768]{1,2,0:T(8,128)(2,1)}, u32[]{:S(2)}) copy-start(bf16[1,384,768]{1,2,0:T(8,128)(2,1)} %copy.39) | copy-start | bytes 1769476
  236.4 5.9 copy-start.47
  311.4 23.7 %collective-permute-start.5 = (bf16[768,768]{1,0:T(8,128)(2,1)}, bf16[768,768]{1,0:T(8,128)(2,1)}, u32[]{:S(2)}, u32[]{:S(2)}) collective-permute-start(bf16[768,768]{1,0:T(8,128)(2,1)} %slice.94), channel_id=1, source_target_pairs={{0,1},{1,0},{2,3},{3,2},{4,5},{5,4},{6,7},{7,6},{8,9},{9,8},{10,11... | collective-permute-start | bytes 3538952 | tf_op jit(solution)/shard_map/ppermute | solution.py:288
  329.6 8.5 %collective-permute-start.6 = (bf16[768,768]{1,0:T(8,128)(2,1)S(1)}, bf16[768,768]{1,0:T(8,128)(2,1)S(1)}, u32[]{:S(2)}, u32[]{:S(2)}) collective-permute-start(bf16[768,768]{1,0:T(8,128)(2,1)S(1)} %slice.96), channel_id=1, source_target_pairs={{0,1},{1,0},{2,3},{3,2},{4,5},{5,4},{6,7},{7,6},{8,9},{9,8},{10,11... | collective-permute-start | bytes 3538952 | tf_op jit(solution)/shard_map/ppermute | solution.py:288
  338.1 8.2 %copy-start.14 = (bf16[768,768]{1,0:T(8,128)(2,1)}, bf16[768,768]{1,0:T(8,128)(2,1)S(1)}, u32[]{:S(2)}) copy-start(bf16[768,768]{1,0:T(8,128)(2,1)S(1)} %collective-permute-done.6) | copy-start | bytes 3538948
  341.3 6.6 %copy-start.30 = (f32[768]{0:T(1024)S(1)}, f32[768]{0:T(1024)}, u32[]{:S(2)}) copy-start(f32[768]{0:T(1024)} %get-tuple-element.32) | copy-start | bytes 9220
  341.3 7.9 %copy-start.31 = (f32[768]{0:T(1024)S(1)}, f32[768]{0:T(1024)}, u32[]{:S(2)}) copy-start(f32[768]{0:T(1024)} %get-tuple-element.26) | copy-start | bytes 9220
  341.3 9.2 %copy-start.44 = (f32[768]{0:T(1024)S(1)}, f32[768]{0:T(1024)}, u32[]{:S(2)}) copy-start(f32[768]{0:T(1024)} %get-tuple-element.62) | copy-start | bytes 9220
  341.3 10.5 %copy-start.32 = (f32[3072]{0:T(1024)S(1)}, f32[3072]{0:T(1024)}, u32[]{:S(2)}) copy-start(f32[3072]{0:T(1024)} %get-tuple-element.64) | copy-start | bytes 36868
  341.3 11.8 %copy-start.2 = (f32[768,768]{0,1:T(8,128)S(1)}, f32[768,768]{0,1:T(8,128)}, u32[]{:S(2)}) copy-start(f32[768,768]{0,1:T(8,128)} %copy-done.1) | copy-start | bytes 7077892
  341.3 11.8 %copy-start.5 = (bf16[1,384,768]{1,2,0:T(8,128)(2,1)S(1)}, bf16[1,384,768]{1,2,0:T(8,128)(2,1)}, u32[]{:S(2)}) copy-start(bf16[1,384,768]{1,2,0:T(8,128)(2,1)} %copy.39) | copy-start | bytes 1769476
  341.3 11.8 %copy-start.19 = (f32[768]{0:T(1024)S(1)}, f32[768]{0:T(1024)}, u32[]{:S(2)}) copy-start(f32[768]{0:T(1024)} %copy-done.18) | copy-start | bytes 9220
  362.2 288.7 %reduce-scatter.2.cloned.1.call-start = ((), (), s32[]{:S(2)}) async-start(), calls=%async_computation.2 | async-start | bytes 14598144 | tf_op jit(solution)/shard_map/reduce_scatter | solution.py:326
  362.3 9.0 %slice-start = ((s8[4718592]{0:T(1024)(128)(4,1)}), s8[4194304]{0:T(1024)(128)(4,1)S(1)}, s32[]{:S(2)}) async-start(s8[4718592]{0:T(1024)(128)(4,1)} %bitcast.29), calls=%async_computation.4 | async-start | bytes 8388608
  369.0 4.8 slice-start.4
  390.2 16.6 %collective-permute-start.3 = (bf16[384,768]{0,1:T(8,128)(2,1)}, bf16[384,768]{0,1:T(8,128)(2,1)S(1)}, u32[]{:S(2)}, u32[]{:S(2)}) collective-permute-start(bf16[384,768]{0,1:T(8,128)(2,1)} %get-tuple-element.45), channel_id=1, source_target_pairs={{0,2},{1,3},{2,0},{3,1},{4,6},{5,7},{6,4},{7,5},{8,10},{9,11},{10,... | collective-permute-start | bytes 1769480 | tf_op jit(solution)/shard_map/ppermute | solution.py:216
  391.7 92.8 %collective-permute-start.7 = (bf16[384,768]{0,1:T(8,128)(2,1)}, bf16[384,768]{0,1:T(8,128)(2,1)S(1)}, u32[]{:S(2)}, u32[]{:S(2)}) collective-permute-start(bf16[384,768]{0,1:T(8,128)(2,1)} %get-tuple-element.41), channel_id=1, source_target_pairs={{0,2},{1,3},{2,0},{3,1},{4,6},{5,7},{6,4},{7,5},{8,10},{9,11},{10,... | collective-permute-start | bytes 1769480 | tf_op jit(solution)/shard_map/ppermute | solution.py:216
  (33 other events, 89.3 us)
Sparse Core Ops, SparseCore 0:
  11.5 108.4 all-gather.1
  362.3 120.7 all-reduce.5
  489.2 161.7 reduce-scatter.1

commit v2 on v1

--- a/solution.py
+++ b/solution.py
@@ -195,7 +195,753 @@
     return tuple(pieces)
 
 
-def local(inputs, lengths, matrices, vectors, cotangent):
+SHARD = 288
+CHUNKS = 3
+CHUNK = SHARD // CHUNKS
+MESH = pl.DeviceIdType.MESH
+UP, DOWN, NEAR_X, NEAR_Y, DIAG_A, DIAG_B, PAIR_C, PAIR_X, PAIR_Y, PAIR_A, PAIR_B = range(11)
+
+
+class Place:
+    def __init__(self):
+        self.seq = lax.axis_index("seq")
+        self.tok = lax.axis_index("tok")
+        self.z = self.seq // 2
+        self.x = self.seq % 2
+        self.y = self.tok // 2
+        self.c = self.tok % 2
+        self.levels = lax.axis_size("seq") // 2
+        self.up = (self.seq + 2, self.tok)
+        self.down = (self.seq - 2, self.tok)
+        self.near_x = (self.seq + 1 - 2 * self.x, self.tok)
+        self.near_y = (self.seq, self.tok + 2 - 4 * self.y)
+        self.pair = (self.seq, self.tok + 1 - 2 * self.c)
+        self.has_up = self.z < self.levels - 1
+        self.has_down = self.z > 0
+
+    def barrier(self):
+        sem = pltpu.get_barrier_semaphore()
+        for device in (self.near_x, self.near_y, self.pair):
+            pl.semaphore_signal(sem, inc=1, device_id=device, device_id_type=MESH)
+
+        @pl.when(self.has_up)
+        def _():
+            pl.semaphore_signal(sem, inc=1, device_id=self.up, device_id_type=MESH)
+
+        @pl.when(self.has_down)
+        def _():
+            pl.semaphore_signal(sem, inc=1, device_id=self.down, device_id_type=MESH)
+
+        count = 3 + self.has_up.astype(jnp.int32) + self.has_down.astype(jnp.int32)
+        pl.semaphore_wait(sem, count)
+
+
+def remote(source, target, send, recv, device):
+    return pltpu.make_async_remote_copy(
+        src_ref=source,
+        dst_ref=target,
+        send_sem=send,
+        recv_sem=recv,
+        device_id=device,
+        device_id_type=MESH,
+    )
+
+
+class Gather:
+    def __init__(self, at, w_ref, send, recv, low, high, split):
+        self.at, self.w, self.send, self.recv = at, w_ref, send, recv
+        self.low, self.high, self.split = low, high, split
+        self.steps = at.levels * CHUNKS + 2
+
+    def piece(self, level, x, y, c, first, count):
+        first = pl.multiple_of(first, 16)
+        return self.w.at[level - self.low, x, y, c, pl.ds(first, count)]
+
+    def copies(self, level, chunk):
+        at, split = self.at, self.split
+        x, y, c = at.x, at.y, at.c
+        first = chunk * CHUNK
+
+        def view(xs, ys, cs, low=0, count=CHUNK):
+            return self.piece(level, xs, ys, cs, first + low, count)
+
+        rest = CHUNK - split
+        table = {
+            UP: (view(x, y, c), view(x, y, c), at.up),
+            DOWN: (view(x, y, c), view(x, y, c), at.down),
+            NEAR_X: (view(x, y, c), view(1 - x, y, c), at.near_x),
+            NEAR_Y: (view(x, y, c), view(x, 1 - y, c), at.near_y),
+            PAIR_C: (view(x, y, c), view(x, y, 1 - c), at.pair),
+            PAIR_X: (view(1 - x, y, c), view(1 - x, y, 1 - c), at.pair),
+            PAIR_Y: (view(x, 1 - y, c), view(x, 1 - y, 1 - c), at.pair),
+        }
+        if split:
+            table[DIAG_A] = (
+                view(1 - x, y, c, 0, split),
+                view(1 - x, 1 - y, c, 0, split),
+                at.near_y,
+            )
+            table[PAIR_A] = (
+                view(1 - x, 1 - y, c, 0, split),
+                view(1 - x, 1 - y, 1 - c, 0, split),
+                at.pair,
+            )
+        if rest:
+            table[DIAG_B] = (
+                view(x, 1 - y, c, split, rest),
+                view(1 - x, 1 - y, c, split, rest),
+                at.near_x,
+            )
+            table[PAIR_B] = (
+                view(1 - x, 1 - y, c, split, rest),
+                view(1 - x, 1 - y, 1 - c, split, rest),
+                at.pair,
+            )
+        return table
+
+    def start(self, table, kind, slot):
+        sent, _, device = table[kind]
+        remote(sent, sent, self.send.at[kind, slot], self.recv.at[kind, slot], device).start()
+
+    def wait_recv(self, table, kind, slot):
+        _, came, device = table[kind]
+        remote(came, came, self.send.at[kind, slot], self.recv.at[kind, slot], device).wait_recv()
+
+    def wait_send(self, table, kind, slot):
+        sent, _, device = table[kind]
+        remote(sent, sent, self.send.at[kind, slot], self.recv.at[kind, slot], device).wait_send()
+
+    def items(self, index, body):
+        at = self.at
+        inside = (index >= 0) & (index < at.levels * CHUNKS)
+        distance = jnp.where(inside, index // CHUNKS, 0)
+        chunk = jnp.where(inside, index % CHUNKS, 0)
+        for below in (True, False):
+            level = at.z - distance if below else at.z + distance
+            valid = inside & (level >= self.low) & (level <= self.high)
+            if not below:
+                valid = valid & (distance > 0)
+
+            @pl.when(valid)
+            def _(level=level, below=below):
+                slot = level * CHUNKS + chunk
+                body(slot, self.copies(level, chunk), distance == 0, below)
+
+    def column(self, index):
+        at = self.at
+
+        def body(slot, table, own, below):
+            @pl.when(jnp.logical_not(own))
+            def _():
+                self.wait_recv(table, UP if below else DOWN, slot)
+
+            if below:
+
+                @pl.when(at.has_up)
+                def _():
+                    self.start(table, UP, slot)
+
+                @pl.when(own & at.has_down)
+                def _():
+                    self.start(table, DOWN, slot)
+
+            else:
+
+                @pl.when(at.has_down)
+                def _():
+                    self.start(table, DOWN, slot)
+
+            for kind in (NEAR_Y, NEAR_X, PAIR_C):
+                self.start(table, kind, slot)
+
+        self.items(index, body)
+
+    def plane(self, index):
+        def body(slot, table, own, below):
+            self.wait_recv(table, NEAR_Y, slot)
+            for kind in (DIAG_B, PAIR_Y):
+                if kind in table:
+                    self.start(table, kind, slot)
+            self.wait_recv(table, NEAR_X, slot)
+            for kind in (DIAG_A, PAIR_X):
+                if kind in table:
+                    self.start(table, kind, slot)
+
+        self.items(index, body)
+
+    def diagonal(self, index):
+        def body(slot, table, own, below):
+            for kind, onward in ((DIAG_B, PAIR_B), (DIAG_A, PAIR_A)):
+                if kind in table:
+                    self.wait_recv(table, kind, slot)
+                    self.start(table, onward, slot)
+
+        self.items(index, body)
+
+    def step(self, number):
+        self.column(number)
+        self.plane(number - 1)
+        self.diagonal(number - 2)
+
+    def finish(self):
+        at = self.at
+
+        def body(slot, table, own, below):
+            for kind in (PAIR_C, PAIR_X, PAIR_Y, PAIR_A, PAIR_B):
+                if kind in table:
+                    self.wait_recv(table, kind, slot)
+            if below:
+
+                @pl.when(at.has_up)
+                def _():
+                    self.wait_send(table, UP, slot)
+
+                @pl.when(own & at.has_down)
+                def _():
+                    self.wait_send(table, DOWN, slot)
+
+            else:
+
+                @pl.when(at.has_down)
+                def _():
+                    self.wait_send(table, DOWN, slot)
+
+            for kind in table:
+                if kind not in (UP, DOWN):
+                    self.wait_send(table, kind, slot)
+
+        def loop(index, carry):
+            self.items(index, body)
+            return carry
+
+        lax.fori_loop(0, at.levels * CHUNKS, loop, 0)
+
+
+class Scatter:
+    def __init__(self, at, g_ref, out_ref, buffers, send, recv, local_sem, low, high):
+        self.at, self.g, self.out, self.send, self.recv = at, g_ref, out_ref, send, recv
+        self.acc, self.from_pair, self.x1, self.y1, self.x2, self.y2, self.za, self.zb = buffers
+        self.local_sem, self.low, self.high = local_sem, low, high
+        self.count = (high - low + 1) * CHUNKS
+        self.last = at.levels + 2
+        self.steps = self.count + self.last
+
+    def half(self):
+        return CHUNK // 2
+
+    def views(self, item):
+        at = self.at
+        x, y, c = at.x, at.y, at.c
+        index = item // CHUNKS
+        first = pl.multiple_of((item % CHUNKS) * CHUNK, 16)
+        h = self.half()
+        rows = pl.ds(first, CHUNK)
+        rows_a = pl.ds(first, h)
+        rows_b = pl.ds(pl.multiple_of(first + h, 16), CHUNK - h)
+        acc = self.acc
+        mine = acc.at[index, x, y, rows]
+        return {
+            0: (self.g.at[index, :, :, 1 - c, rows], self.from_pair.at[index, :, :, rows], at.pair),
+            1: (acc.at[index, 1 - x, :, rows_a], self.x1.at[item], at.near_x),
+            2: (acc.at[index, :, 1 - y, rows_b], self.y1.at[item], at.near_y),
+            3: (acc.at[index, x, 1 - y, rows_a], self.y2.at[item], at.near_y),
+            4: (acc.at[index, 1 - x, y, rows_b], self.x2.at[item], at.near_x),
+            5: (mine, self.zb.at[item], at.up),
+            6: (mine, self.za.at[item], at.down),
+        }, index, (rows, rows_a, rows_b)
+
+    def copy(self, views, kind, item):
+        source, target, device = views[kind]
+        return remote(source, target, self.send.at[kind, item], self.recv.at[kind, item], device)
+
+    def guarded(self, item, body, extra=None):
+        valid = (item >= 0) & (item < self.count)
+        item = jnp.where(valid, item, 0)
+        level = self.low + item // CHUNKS
+        if extra is not None:
+            valid = valid & extra(level)
+
+        @pl.when(valid)
+        def _():
+            views, index, rows = self.views(item)
+            body(item, views, index, rows)
+
+    def local(self, item, index, rows):
+        return pltpu.make_async_copy(
+            self.g.at[index, :, :, self.at.c, rows[0]],
+            self.acc.at[index, :, :, rows[0]],
+            self.local_sem.at[item],
+        )
+
+    def begin(self, item):
+        def body(item, views, index, rows):
+            self.copy(views, 0, item).start()
+            self.local(item, index, rows).start()
+
+        self.guarded(item, body)
+
+    @staticmethod
+    def add(target, where, addend):
+        target[where] = (target[where].astype(F32) + addend.astype(F32)).astype(BF16)
+
+    def first(self, item):
+        def body(item, views, index, rows):
+            self.copy(views, 0, item).wait_recv()
+            self.local(item, index, rows).wait()
+            for xs in range(2):
+                for ys in range(2):
+                    where = (index, xs, ys, rows[0])
+                    self.add(self.acc, where, self.from_pair[where])
+            self.copy(views, 1, item).start()
+            self.copy(views, 2, item).start()
+
+        self.guarded(item, body)
+
+    def second(self, item):
+        at = self.at
+
+        def body(item, views, index, rows):
+            self.copy(views, 1, item).wait_recv()
+            for ys in range(2):
+                self.add(self.acc, (index, at.x, ys, rows[1]), self.x1[item, ys])
+            self.copy(views, 3, item).start()
+            self.copy(views, 2, item).wait_recv()
+            for xs in range(2):
+                self.add(self.acc, (index, xs, at.y, rows[2]), self.y1[item, xs])
+            self.copy(views, 4, item).start()
+
+        self.guarded(item, body)
+
+    def collect(self, item, views, index, rows):
+        at = self.at
+        self.copy(views, 3, item).wait_recv()
+        self.copy(views, 4, item).wait_recv()
+        self.add(self.acc, (index, at.x, at.y, rows[1]), self.y2[item])
+        self.add(self.acc, (index, at.x, at.y, rows[2]), self.x2[item])
+
+    def along(self, step):
+        at = self.at
+
+        def rise(item, views, index, rows):
+            self.collect(item, views, index, rows)
+
+            @pl.when(at.has_down)
+            def _():
+                self.copy(views, 5, item).wait_recv()
+                self.add(self.acc, (index, at.x, at.y, rows[0]), self.zb[item])
+
+            self.copy(views, 5, item).start()
+
+        def sink(item, views, index, rows):
+            self.collect(item, views, index, rows)
+
+            @pl.when(at.has_up)
+            def _():
+                self.copy(views, 6, item).wait_recv()
+                self.add(self.acc, (index, at.x, at.y, rows[0]), self.za[item])
+
+            self.copy(views, 6, item).start()
+
+        def arrive(item, views, index, rows):
+            self.collect(item, views, index, rows)
+            self.out[rows[0]] = self.acc[index, at.x, at.y, rows[0]].astype(F32)
+
+            @pl.when(at.has_down)
+            def _():
+                self.copy(views, 5, item).wait_recv()
+                self.out[rows[0]] = self.out[rows[0]] + self.zb[item].astype(F32)
+
+            @pl.when(at.has_up)
+            def _():
+                self.copy(views, 6, item).wait_recv()
+                self.out[rows[0]] = self.out[rows[0]] + self.za[item].astype(F32)
+
+        top = at.levels - 1
+        self.guarded(step - 3 - at.z, rise, lambda level: level > at.z)
+        self.guarded(step - 3 - (top - at.z), sink, lambda level: level < at.z)
+        self.guarded(step - self.last, arrive, lambda level: level == at.z)
+
+    def step(self, number):
+        self.begin(number)
+        self.first(number - 1)
+        self.second(number - 2)
+        self.along(number)
+
+    def finish(self):
+        at = self.at
+
+        def loop(item, carry):
+            def body(item, views, index, rows):
+                for kind in range(5):
+                    self.copy(views, kind, item).wait_send()
+
+            self.guarded(item, body)
+            self.guarded(
+                item,
+                lambda item, views, index, rows: self.copy(views, 5, item).wait_send(),
+                lambda level: level > at.z,
+            )
+            self.guarded(
+                item,
+                lambda item, views, index, rows: self.copy(views, 6, item).wait_send(),
+                lambda level: level < at.z,
+            )
+            return carry
+
+        lax.fori_loop(0, self.count, loop, 0)
+
+
+class Total:
+    def __init__(self, at, sums, came, send, recv):
+        self.at, self.sums, self.came, self.send, self.recv = at, sums, came, send, recv
+        self.steps = 4 + at.levels
+
+    def copy(self, kind, slot, device):
+        return remote(
+            self.sums.at[slot], self.came.at[kind], self.send.at[kind], self.recv.at[kind], device
+        )
+
+    def near(self, kind):
+        at = self.at
+        return self.copy(kind, kind, (at.pair, at.near_x, at.near_y)[kind])
+
+    def sink(self):
+        return self.copy(3, 4, self.at.down)
+
+    def rise(self):
+        return self.copy(4, 5, self.at.up)
+
+    def step(self, number):
+        at = self.at
+        top = at.levels - 1
+        for kind in range(3):
+
+            @pl.when(number == kind)
+            def _(kind=kind):
+                if kind:
+                    self.near(kind - 1).wait_recv()
+                    self.sums[kind] = self.sums[kind - 1] + self.came[kind - 1]
+                self.near(kind).start()
+
+        @pl.when(number == 3)
+        def _():
+            self.near(2).wait_recv()
+            total = self.sums[2] + self.came[2]
+            self.sums[3] = total
+            self.sums[4] = total
+            self.sums[5] = total
+
+        @pl.when((number == 4 + top - at.z) & at.has_down)
+        def _():
+            @pl.when(at.has_up)
+            def _():
+                self.sink().wait_recv()
+                self.sums[4] = self.sums[3] + self.came[3]
+
+            self.sink().start()
+
+        @pl.when((number == 4 + at.z) & at.has_up)
+        def _():
+            @pl.when(at.has_down)
+            def _():
+                self.rise().wait_recv()
+                self.sums[5] = self.sums[3] + self.came[4]
+
+            self.rise().start()
+
+    def finish(self, out_ref):
+        at = self.at
+
+        @pl.when(jnp.logical_not(at.has_down))
+        def _():
+            self.sink().wait_recv()
+
+        @pl.when(jnp.logical_not(at.has_up))
+        def _():
+            self.rise().wait_recv()
+
+        out_ref[...] = self.sums[3]
+
+        @pl.when(at.has_up)
+        def _():
+            out_ref[...] = out_ref[...] + self.came[3]
+            self.rise().wait_send()
+
+        @pl.when(at.has_down)
+        def _():
+            out_ref[...] = out_ref[...] + self.came[4]
+            self.sink().wait_send()
+
+        for kind in range(3):
+            self.near(kind).wait_send()
+
+
+def total_scratch(rows):
+    return [
+        pltpu.VMEM((6, rows, 128), F32),
+        pltpu.VMEM((5, rows, 128), F32),
+        pltpu.SemaphoreType.DMA((5,)),
+        pltpu.SemaphoreType.DMA((5,)),
+    ]
+
+
+def scatter_scratch(levels):
+    items = levels * CHUNKS
+    h = CHUNK // 2
+    return [
+        pltpu.VMEM((levels, 2, 2, SHARD, D), BF16),
+        pltpu.VMEM((levels, 2, 2, SHARD, D), BF16),
+        pltpu.VMEM((items, 2, h, D), BF16),
+        pltpu.VMEM((items, 2, CHUNK - h, D), BF16),
+        pltpu.VMEM((items, CHUNK - h, D), BF16),
+        pltpu.VMEM((items, h, D), BF16),
+        pltpu.VMEM((items, CHUNK, D), BF16),
+        pltpu.VMEM((items, CHUNK, D), BF16),
+        pltpu.SemaphoreType.DMA((7, items)),
+        pltpu.SemaphoreType.DMA((7, items)),
+        pltpu.SemaphoreType.DMA((items,)),
+    ]
+
+
+def vector_row(vec_ref, first, count=D):
+    low = first // 128
+    return jnp.concatenate([vec_ref[low + i : low + i + 1, :] for i in range(count // 128)], axis=1)
+
+
+def rows_of(ref, first, count):
+    return ref[...].reshape(-1, D)[first : first + count]
+
+
+ROW_CHUNK = 256
+
+
+def forward_call_kernel(
+    own_ref,
+    vec_ref,
+    in_ref,
+    bias_ref,
+    x_ref,
+    n_ref,
+    q_ref,
+    k_ref,
+    v_ref,
+    o_ref,
+    lt_ref,
+    w0_ref,
+    w1_ref,
+    vecs_ref,
+    l_ref,
+    send0,
+    recv0,
+    send1,
+    recv1,
+    misc_send,
+    misc_recv,
+    local_sem,
+    *vec_scratch,
+):
+    at = Place()
+    rows = x_ref.shape[0]
+    slots = rows // 2
+    kept = pltpu.make_async_copy(in_ref.at[at.y], x_ref.at[pl.ds(0, slots)], local_sem.at[0])
+    kept.start()
+
+    def own_copy():
+        first = pltpu.make_async_copy(own_ref, w0_ref.at[0, at.x, at.y, at.c], local_sem.at[1])
+        later = pltpu.make_async_copy(
+            own_ref, w1_ref.at[jnp.maximum(at.z - 1, 0), at.x, at.y, at.c], local_sem.at[1]
+        )
+        return first, later
+
+    first_own, later_own = own_copy()
+
+    @pl.when(at.z == 0)
+    def _():
+        first_own.start()
+
+    @pl.when(at.z > 0)
+    def _():
+        later_own.start()
+
+    sums, came, vec_send, vec_recv = vec_scratch
+    sums[0] = vec_ref[...]
+    total = Total(at, sums, came, vec_send, vec_recv)
+    first_own.wait()
+    at.barrier()
+
+    swap = remote(
+        in_ref.at[1 - at.y],
+        x_ref.at[pl.ds(slots, slots)],
+        misc_send.at[0],
+        misc_recv.at[0],
+        at.near_y,
+    )
+    base = Gather(at, w0_ref, send0, recv0, 0, 0, 0)
+    rest = Gather(at, w1_ref, send1, recv1, 1, at.levels - 1, 48)
+
+    total.step(0)
+    swap.start()
+    for number in range(3):
+        base.step(number)
+    kept.wait()
+
+    def early(number, carry):
+        base.step(number)
+        total.step(number - 2)
+        return carry
+
+    lax.fori_loop(3, 10, early, 0)
+    total.step(8)
+    total.finish(vecs_ref)
+    for number in range(3):
+        rest.column(number)
+    swap.wait_recv()
+    gain = vector_row(vecs_ref, 0)
+    shift = vector_row(vecs_ref, D)
+    for chunk in range(rows // ROW_CHUNK):
+        part = pl.ds(chunk * ROW_CHUNK, ROW_CHUNK)
+        n_ref[part, :] = layer_norm(x_ref[part, :].astype(F32), gain, shift).astype(BF16)
+
+    def late(number, carry):
+        base.step(number)
+        return carry
+
+    lax.fori_loop(10, base.steps, late, 0)
+    base.finish()
+
+    bias_query = vector_row(vecs_ref, 2 * D)
+    bias_value = vector_row(vecs_ref, 3 * D)
+    w_key = rows_of(w0_ref, D, D)
+    for chunk in range(rows // ROW_CHUNK):
+        part = pl.ds(chunk * ROW_CHUNK, ROW_CHUNK)
+        k_ref[part, :] = matmul(n_ref[part, :], w_key).astype(BF16)
+    mine, other = pl.ds(0, rows), pl.ds(rows, rows)
+    key_copy = remote(k_ref.at[mine], k_ref.at[other], misc_send.at[1], misc_recv.at[1], at.pair)
+    value_copy = remote(v_ref.at[mine], v_ref.at[other], misc_send.at[2], misc_recv.at[2], at.pair)
+    key_copy.start()
+    w_value = rows_of(w0_ref, 2 * D, D)
+    for chunk in range(rows // ROW_CHUNK):
+        part = pl.ds(chunk * ROW_CHUNK, ROW_CHUNK)
+        v_ref[part, :] = (matmul(n_ref[part, :], w_value) + bias_value).astype(BF16)
+    value_copy.start()
+    w_query = rows_of(w0_ref, 0, D)
+    for chunk in range(rows // ROW_CHUNK):
+        part = pl.ds(chunk * ROW_CHUNK, ROW_CHUNK)
+        query = (matmul(n_ref[part, :], w_query) + bias_query).astype(BF16)
+        q_ref[part, :] = query * jnp.asarray(HEAD ** (-0.5), BF16)
+    rest.plane(0)
+    l_ref[...] = jnp.zeros_like(l_ref)
+    key_copy.wait_recv()
+    value_copy.wait_recv()
+
+    def pair_step(pair, carry):
+        forward_pair(pair, q_ref, k_ref, v_ref, bias_ref, o_ref, l_ref, ROW_CHUNK)
+        for extra in range(2):
+            number = 2 * pair + extra + 1
+
+            @pl.when(number > 2)
+            def _(number=number):
+                rest.column(number)
+
+            rest.plane(number - 0)
+            rest.diagonal(number - 1)
+        return carry
+
+    def rest_step(number, carry):
+        rest.column(number)
+        rest.plane(number)
+        rest.diagonal(number - 1)
+        return carry
+
+    lax.fori_loop(0, PAIRS, pair_step, 0)
+    lt_ref[...] = l_ref[...].T[: lt_ref.shape[0]]
+    lax.fori_loop(2 * PAIRS + 1, rest.steps, rest_step, 0)
+    rest.finish()
+    swap.wait_send()
+    key_copy.wait_send()
+    value_copy.wait_send()
+
+
+def forward_call(own, vec_part, inputs, bias, levels):
+    rows = inputs.shape[0] * inputs.shape[1]
+    vmem = pl.BlockSpec(memory_space=pltpu.VMEM)
+    anywhere = pl.BlockSpec(memory_space=pl.ANY)
+    slots = levels * CHUNKS
+    low = lambda *shape: jax.ShapeDtypeStruct(shape, BF16)
+    return pl.pallas_call(
+        forward_call_kernel,
+        out_shape=(
+            low(rows, D),
+            low(rows, D),
+            low(rows, D),
+            low(2 * rows, D),
+            low(2 * rows, D),
+            low(rows, D),
+            jax.ShapeDtypeStruct((16, rows), F32),
+            low(1, 2, 2, 2, SHARD, D),
+            low(levels - 1, 2, 2, 2, SHARD, D),
+            jax.ShapeDtypeStruct(vec_part.shape, F32),
+        ),
+        in_specs=[anywhere, vmem, anywhere, vmem],
+        out_specs=(vmem,) * 8 + (anywhere, vmem),
+        scratch_shapes=[
+            pltpu.VMEM((rows, LANES), F32),
+            pltpu.SemaphoreType.DMA((11, slots)),
+            pltpu.SemaphoreType.DMA((11, slots)),
+            pltpu.SemaphoreType.DMA((11, slots)),
+            pltpu.SemaphoreType.DMA((11, slots)),
+            pltpu.SemaphoreType.DMA((3,)),
+            pltpu.SemaphoreType.DMA((3,)),
+            pltpu.SemaphoreType.DMA((2,)),
+        ]
+        + total_scratch(vec_part.shape[0]),
+        compiler_params=pltpu.CompilerParams(
+            collective_id=0, has_side_effects=True, vmem_limit_bytes=VMEM_LIMIT
+        ),
+        name="gather_attend",
+    )(own, vec_part, inputs, bias)
+
+
+def scatter_call_kernel(g_ref, vec_ref, out_ref, vecs_ref, *scratch):
+    at = Place()
+    sums, came, vec_send, vec_recv = scratch[11:]
+    sums[0] = vec_ref[...]
+    at.barrier()
+    total = Total(at, sums, came, vec_send, vec_recv)
+    scatter = Scatter(
+        at, g_ref, out_ref, scratch[:8], scratch[8], scratch[9], scratch[10], 0, at.levels - 1
+    )
+
+    def step(number, carry):
+        scatter.step(number)
+        total.step(number)
+        return carry
+
+    lax.fori_loop(0, scatter.steps, step, 0)
+    total.finish(vecs_ref)
+    scatter.finish()
+
+
+def scatter_call(grads, vec_part, levels):
+    vmem = pl.BlockSpec(memory_space=pltpu.VMEM)
+    anywhere = pl.BlockSpec(memory_space=pl.ANY)
+    return pl.pallas_call(
+        scatter_call_kernel,
+        out_shape=(
+            jax.ShapeDtypeStruct((SHARD, D), F32),
+            jax.ShapeDtypeStruct(vec_part.shape, F32),
+        ),
+        in_specs=[anywhere, vmem],
+        out_specs=(vmem, vmem),
+        scratch_shapes=scatter_scratch(levels) + total_scratch(vec_part.shape[0]),
+        compiler_params=pltpu.CompilerParams(
+            collective_id=1, has_side_effects=True, vmem_limit_bytes=VMEM_LIMIT
+        ),
+        name="scatter_sum",
+    )(grads, vec_part)
+
+
+def plain_local(inputs, lengths, matrices, vectors, cotangent):
     seq_count, local_slots, width = inputs.shape
     tok_size = lax.axis_size("tok")
     tok = lax.axis_index("tok")
@@ -334,7 +1080,143 @@
     return (outputs, grad_inputs, grad_matrices, grad_vectors)
 
 
+def fast_local(inputs, lengths, matrices, vectors, cotangent):
+    seq_count, local_slots, width = inputs.shape
+    tok = lax.axis_index("tok")
+    half = tok // 2
+    place = lax.axis_index("seq") * lax.axis_size("tok") + tok
+    levels = lax.axis_size("seq") // 2
+    devices = lax.axis_size("seq") * lax.axis_size("tok")
+    rows = seq_count * local_slots
+    across = [(i, (i + 2) % 4) for i in range(4)]
+    partner = [(i, i + 1 - 2 * (i % 2)) for i in range(4)]
+
+    def pick(array, index):
+        return lax.dynamic_index_in_dim(array, index, 0, keepdims=False)
+
+    def to_sequence(array):
+        other = lax.ppermute(pick(array, 1 - half), "tok", across)
+        return jnp.concatenate([pick(array, half), other], axis=0)
+
+    def from_sequence(array):
+        other = lax.ppermute(array[local_slots:], "tok", across)
+        kept = array[:local_slots]
+        return jnp.where(half == 0, jnp.stack([kept, other]), jnp.stack([other, kept]))
+
+    own = matrices.reshape(SHARD, width).astype(BF16)
+    vec_count = vectors.shape[0]
+    vec_total = vec_count * devices
+    vec_part = lax.dynamic_update_slice(
+        jnp.zeros((vec_total,), F32), vectors.astype(BF16).astype(F32), (place * vec_count,)
+    ).reshape(vec_total // 128, 128)
+    length = pick(lengths, half)
+    slot = jnp.arange(local_slots, dtype=jnp.int32)
+    places = jnp.concatenate(
+        [block * local_slots + slot for block in (tok, tok ^ 2, tok ^ 1, tok ^ 3)]
+    )
+    bias = jnp.where(places < length, 0.0, -1e30).astype(BF16)[:, None]
+    bias = jnp.broadcast_to(bias, (bias.shape[0], LANES))
+    frames, normed, scaled, keys, values, attended, lt, w_first, w_rest, vecs = forward_call(
+        own, vec_part, inputs, bias, levels
+    )
+    grad_out = to_sequence(cotangent)
+    (
+        gain_one,
+        first_norm_shift,
+        bias_query,
+        bias_value,
+        bias_out,
+        gain_two,
+        shift_two,
+        bias_up,
+        bias_down,
+    ) = split_vectors(vecs.reshape(-1))
+    first_rows = w_first.reshape(-1, width)
+    w_query, w_key, w_value = (first_rows[i * D : (i + 1) * D] for i in range(3))
+    rest_rows = w_rest.reshape(-1, width)
+    w_out = rest_rows[:D]
+    w_up = rest_rows[D : D + FF].reshape(D, FF)
+    w_down = rest_rows[D + FF : D + 2 * FF]
+    token_rows = frames.astype(F32)
+    middle = token_rows + (matmul(attended, w_out) + bias_out)
+    normed_two = layer_norm(middle, gain_two, shift_two).astype(BF16)
+    hidden = matmul(normed_two, w_up) + bias_up
+    active = jax.nn.gelu(hidden, approximate=False).astype(BF16)
+    result = middle + (matmul(active, w_down) + bias_down)
+    outputs = from_sequence(result.astype(BF16))
+
+    grad_out_wide = grad_out.astype(F32)
+    d_down = outer_sum(active, grad_out)
+    down_bias_gradient = column_sum(grad_out)
+    grad_active = back_product(grad_out, w_down)
+    gelu_value, gelu_pull = jax.vjp(partial(jax.nn.gelu, approximate=False), hidden)
+    grad_hidden = gelu_pull(grad_active)[0].astype(BF16)
+    d_up = outer_sum(normed_two, grad_hidden)
+    d_bias_up = column_sum(grad_hidden)
+    grad_normed_two = back_product(grad_hidden, w_up)
+    norm_value, norm_pull = jax.vjp(layer_norm, middle, gain_two, shift_two)
+    grad_mid_norm, d_gain_two, d_shift_two = norm_pull(grad_normed_two)
+    grad_middle = grad_out_wide + grad_mid_norm
+    grad_branch = grad_middle.astype(BF16)
+    d_out = outer_sum(attended, grad_branch)
+    d_bias_out = column_sum(grad_branch)
+    grad_attended = back_product(grad_branch, w_out).astype(BF16)
+    inner = (grad_attended.astype(F32) * attended.astype(F32)).reshape(rows, HEADS, HEAD).sum(-1)
+    inner = jnp.pad(inner.T, ((0, 16 - HEADS), (0, 0)))
+    grad_query, grad_keys, grad_values = attend_back(
+        scaled, keys, values, bias, grad_attended, lt, inner
+    )
+
+    def pair_sum(array):
+        other = lax.ppermute(array[rows:], "tok", partner)
+        return (array[:rows].astype(F32) + other.astype(F32)).astype(BF16)
+
+    grad_key = pair_sum(grad_keys)
+    grad_value = pair_sum(grad_values)
+    d_query = outer_sum(normed, grad_query)
+    d_key = outer_sum(normed, grad_key)
+    d_value = outer_sum(normed, grad_value)
+    d_bias_query = column_sum(grad_query)
+    d_bias_value = column_sum(grad_value)
+    grad_normed = (
+        back_product(grad_query, w_query)
+        + back_product(grad_key, w_key)
+        + back_product(grad_value, w_value)
+    )
+    first_value, leading_pullback = jax.vjp(layer_norm, token_rows, gain_one, first_norm_shift)
+    grad_rows_norm, d_gain_one, d_shift_one = leading_pullback(grad_normed)
+    grad_inputs = from_sequence((grad_middle + grad_rows_norm).astype(BF16))
+    matrix_rows = jnp.concatenate(
+        [
+            piece.astype(BF16).reshape(-1, width)
+            for piece in (d_query, d_key, d_value, d_out, d_up, d_down)
+        ]
+    )
+    flat_vector_grads = jnp.concatenate(
+        [
+            d_gain_one,
+            d_shift_one,
+            d_bias_query,
+            d_bias_value,
+            d_bias_out,
+            d_gain_two,
+            d_shift_two,
+            d_bias_up,
+            down_bias_gradient,
+        ]
+    )
+    grad_rows, grad_vecs = scatter_call(
+        matrix_rows.reshape(levels, 2, 2, 2, SHARD, width),
+        flat_vector_grads.reshape(vec_part.shape),
+        levels,
+    )
+    grad_matrices = grad_rows.reshape(-1)
+    grad_vectors = lax.dynamic_slice(grad_vecs.reshape(-1), (place * vec_count,), (vec_count,))
+    return (outputs, grad_inputs, grad_matrices, grad_vectors)
+
+
 def solution(mesh):
+    seq_size, tok_size = mesh.shape["seq"], mesh.shape["tok"]
     in_specs = (
         P("seq", "tok", None),
         P("seq"),
@@ -343,4 +1225,6 @@
         P("seq", "tok", None),
     )
     out_specs = (P("seq", "tok", None), P("seq", "tok", None), P(("seq", "tok")), P(("seq", "tok")))
-    return jax.shard_map(local, mesh=mesh, in_specs=in_specs, out_specs=out_specs, check_vma=False)
+    whole_rows = (4 * D + 2 * FF) == seq_size * tok_size * SHARD
+    body = fast_local if whole_rows and tok_size == 4 else plain_local
+    return jax.shard_map(body, mesh=mesh, in_specs=in_specs, out_specs=out_specs, check_vma=False)

time: 667 us -> 460 us (0.69)
  the two profiles are of different devices: /device:TPU:0 before, /device:TPU:24 now
where the time goes in v2:
time: 460 us; the launch traced here: 456 us
  Pallas kernels  291 us (63%)
  matrix products  95.3 us (21%)
  local copies, waits for them, and re-layouts  46.6 us (10%)
  other arithmetic  16.8 us (4%)
    pallas_call x1, Pallas kernels, forward_call(): pl.pallas_call(forward_call_kernel, out_shape=(low(rows, D), low(rows, D)...  166 us
    pallas_call x1, Pallas kernels, scatter_call(): pl.pallas_call(scatter_call_kernel, out_shape=(jax.ShapeDtypeStruct((SHAR...  79.8 us
    pallas_call x1, Pallas kernels, attend_back(): pl.pallas_call(partial(backward_kernel, 256), out_shape=(jax.ShapeDtypeSt...  45.3 us
    dot_general x3, matrix products, matmul(): return jnp.dot(left_operand, right_operand, preferred_element_type=F32)  38.6 us
    dot_general x6, matrix products, back_product(): lax.dot_general(gradient, weight, (((1,), (1,)), ((), ())), preferred_ele...  31.5 us
    dot_general x6, matrix products, outer_sum(): lax.dot_general(left_operand, right_operand, (((0,), (0,)), ((), ())), pr...  25.2 us
  transfers between devices with their start and end apart: 5, of which 0 were waited for; matrix products, arithmetic and copies ran while one was open for 33% of the time, Pallas kernels for 64%

profile of v2, /device:TPU:24, one launch (start us, length us, event | category | flops | bytes accessed | tf_op | source)
XLA Modules:
  0.0 455.7 jit_solution(10125327109687177346)
XLA Ops:
  0.7 2.4 dynamic-slice_bitcast_fusion.1
  3.1 1.5 collective-permute-start.1
  8.3 166.3 %gather_attend.1 = (bf16[768,768]{1,0:T(8,128)(2,1)}, bf16[768,768]{1,0:T(8,128)(2,1)}, bf16[768,768]{1,0:T(8,128)(2,1)}, bf16[1536,768]{1,0:T(8,128)(2,1)}, bf1...) custom-call(bf16[288,768]{1,0:T(8,128)(2,1)} %convert_element_type.1, ...), custom_call_target="tpu_custom_call" | custom-call | tf_op jit(solution)/shard_map/gather_attend/pallas_call | solution.py:871
  177.3 5.0 %slice.87 = bf16[3072,768]{1,0:T(8,128)(2,1)} slice(bf16[6912,768]{1,0:T(8,128)(2,1)} %bitcast.49), slice={[768:3840], [0:768]} | slice | bytes 9437184 | tf_op jit(solution)/shard_map/slice | solution.py:1138
  182.3 2.5 fusion.43
  186.0 8.5 %reshape.148 = bf16[768,3072]{1,0:T(8,128)(2,1)} reshape(bf16[3072,768]{1,0:T(8,128)(2,1)} %slice.87) | data formatting | bytes 9437184 | tf_op jit(solution)/shard_map/reshape | solution.py:1138
  194.5 28.2 %multiply_convert_fusion = (bf16[768,3072]{1,0:T(8,128)(2,1)S(1)}, f32[768,3072]{1,0:T(8,128)}, f32[768,3072]{1,0:T(8,128)}) fusion(f32[3072]{0:T(1024)} %slice_bitcast_fusion.2, bf16[768,3072]{1,0:T(8,128)(2,1)} %reshape.148, f32[768,768]{1,0:T(8,128)S(1)} %get-tuple-element.64, f32[768]{0:T(1024)} %get-tuple-element.58, f32[768]{0:T(1024)S(1)} %get-tuple-element.59, ...), kind=kOutput, calls=%fused_computation.4 | convolution fusion | flops 3782541312 | bytes 30695424 | tf_op jit(solution)/shard_map/dot_general | solution.py:29
  222.8 7.9 %add_convert_fusion.4 = bf16[768,768]{1,0:T(8,128)(2,1)S(1)} fusion(f32[768,768]{1,0:T(8,128)S(1)} %get-tuple-element.64, bf16[768,3072]{1,0:T(8,128)(2,1)S(1)} %get-tuple-element.46, bf16[6912,768]{1,0:T(8,128)(2,1)} %bitcast.51, f32[768]{0:T(1024)S(1)} %copy-done.26), kind=kOutput, calls=%fused_computation.50 | convolution fusion | flops 3625648128 | bytes 12979200 | tf_op jit(solution)/shard_map/dot_general | solution.py:29
  233.0 12.7 %convert_reduce_fusion = (f32[3072]{0:T(1024)}, bf16[768,3072]{1,0:T(8,128)(2,1)S(1)}) fusion(f32[768,3072]{1,0:T(8,128)} %get-tuple-element.47, bf16[6912,768]{1,0:T(8,128)(2,1)} %bitcast.52, bf16[384,768]{1,0:T(8,128)(2,1)} %collective-permute-done.1, bf16[384,768]{1,0:T(8,128)(2,1)} %get-tuple-element.52, f32[768,3072]{1,0:T(8,128)} %get-tuple-element.65, ...), kind=kOutput, calls=%fused_computation.2 | convolution fusion | flops 3666342912 | bytes 29515776 | tf_op jit(solution)/shard_map/dot_general | solution.py:39
  245.7 9.0 %multiply_reduce_fusion = (f32[768]{0:T(1024)}, f32[768]{0:T(1024)S(1)}, f32[768]{0:T(1024)}, f32[768,768]{1,0:T(8,128)S(1)}) fusion(f32[768,768]{1,0:T(8,128)S(1)} %get-tuple-element.64, f32[768]{0:T(1024)S(1)} %copy-done.22, f32[768]{0:T(1024)S(1)} %broadcast_multiply_fusion.1, f32[768]{0:T(1024)S(1)} %copy-done.19, ...), kind=kOutput, calls=%fused_computation.40 | convolution fusion | flops 3628594944 | bytes 14174208 | tf_op jit(solution)/shard_map/dot_general | solution.py:39
  254.7 2.6 fusion.41
  257.3 2.2 convert_reduce_fusion.3
  259.5 4.6 %convert_multiply_fusion = (f32[768,768]{1,0:T(8,128)}, bf16[768,768]{1,0:T(8,128)(2,1)}) fusion(bf16[768,768]{1,0:T(8,128)(2,1)S(1)} %copy-done.10, bf16[768,768]{1,0:T(8,128)(2,1)S(1)} %get-tuple-element.43, bf16[6912,768]{1,0:T(8,128)(2,1)} %bitcast.53), kind=kOutput, calls=%fused_computation.48 | convolution fusion | flops 908328960 | bytes 7077888 | tf_op jit(solution)/shard_map/dot_general | solution.py:39
  264.1 3.1 copy.13
  267.2 2.5 reduce_sum.163
  271.1 45.3 %attend_back.1 = (bf16[768,768]{1,0:T(8,128)(2,1)}, bf16[1536,768]{1,0:T(8,128)(2,1)}, bf16[1536,768]{1,0:T(8,128)(2,1)}) custom-call(bf16[768,768]{1,0:T(8,128)(2,1)} %get-tuple-element.23.refs_0_, bf16[1536,768]{1,0:T(8,128)(2,1)} %get-tuple-element.24.refs_1_, bf16[1536,768]{1,0:T(8,128)(2,1)} %get-tuple-element.25.refs_2_, ...), custom_call_target="tpu_custom_call" | custom-call | tf_op jit(solution)/shard_map/attend_back/pallas_call | solution.py:169
  316.3 2.5 slice.78
  318.9 8.2 %convolution_convert_fusion.1 = bf16[768,3072]{1,0:T(8,128)(2,1)} fusion(bf16[768,3072]{1,0:T(8,128)(2,1)} %copy-done.33, f32[768,768]{1,0:T(8,128)S(1)} %copy-done.2, f32[768]{0:T(1024)S(1)} %copy-done.25, f32[768]{0:T(1024)S(1)} %copy-done.20, f32[768]{0:T(1024)S(1)} %copy-done.23, f32[768]{0:T(1024)S(1)} %broadcast_multiply_fusion.1), kind=kOutput, calls=%fused_computation.20 | convolution fusion | flops 3629187072 | bytes 11808768 | tf_op jit(solution)/shard_map/dot_general | solution.py:33
  327.1 8.6 %reshape.151 = bf16[3072,768]{1,0:T(8,128)(2,1)} reshape(bf16[768,3072]{1,0:T(8,128)(2,1)} %convolution_convert_fusion.1) | data formatting | bytes 9437184 | tf_op jit(solution)/shard_map/reshape | solution.py:1191
  335.8 1.5 slice.81
  338.1 2.4 maximum_select_fusion
  340.5 2.2 fusion.26
  344.3 2.6 fusion.29
  346.9 1.6 fusion.39
  349.7 1.9 convert_reduce_fusion.2
  352.8 3.4 fusion.25
  356.2 2.2 fusion.24
  358.4 2.2 fusion.23
  361.4 2.5 constant_dynamic-update-slice_fusion
  363.9 7.1 %fusion.6 = bf16[9216,768]{1,0:T(8,128)(2,1)} fusion(bf16[9216,768]{1,0:T(8,128)(2,1)} %constant_dynamic-update-slice_fusion, bf16[768,3072]{1,0:T(8,128)(2,1)S(1)} %bitcast.63, bf16[384,768]{1,0:T(8,128)(2,1)} %collective-permute-done.1, bf16[384,768]{1,0:T(8,128)(2,1)S(1)} %copy-done.4), kind=kOutput, calls=%fused_computation.19 | convolution fusion | flops 3628597248 | bytes 10616832 | tf_op jit(solution)/shard_map/dot_general | solution.py:33
  371.0 79.8 %scatter_sum.1 = (f32[288,768]{1,0:T(8,128)}, f32[72,128]{1,0:T(8,128)}) custom-call(bf16[4,2,2,2,288,768]{5,4,3,2,1,0:T(8,128)(2,1)} %bitcast.18.g_ref, f32[72,128]{1,0:T(8,128)} %bitcast.57), custom_call_target="tpu_custom_call" | custom-call | tf_op jit(solution)/shard_map/scatter_sum/pallas_call | solution.py:928
  450.8 2.1 reshape.154
  (128 shorter events, 19.4 us)
Async XLA Ops:
  0.6 4.0 copy-start.32
  0.6 4.6 %copy-start.13 = (f32[221184]{0:T(1024)S(1)}, f32[221184]{0:T(1024)}, u32[]{:S(2)}) copy-start(f32[221184]{0:T(1024)} %param.7) | copy-start | bytes 2654212
  0.7 5.8 %copy-start.29 = (f32[288]{0:T(512)S(1)}, f32[288]{0:T(512)}, u32[]{:S(2)}) copy-start(f32[288]{0:T(512)} %param.8) | copy-start | bytes 3460
  3.1 229.9 %collective-permute-start.1 = (bf16[384,768]{1,0:T(8,128)(2,1)}, bf16[384,768]{1,0:T(8,128)(2,1)}, u32[]{:S(2)}, u32[]{:S(2)}) collective-permute-start(bf16[384,768]{1,0:T(8,128)(2,1)} %get-tuple-element.53), channel_id=1, source_target_pairs={{0,2},{1,3},{2,0},{3,1},{4,6},{5,7},{6,4},{7,5},{8,10},{9,11},{10,... | collective-permute-start | bytes 1769480 | tf_op jit(solution)/shard_map/ppermute | solution.py:1098
  177.3 17.3 %copy-start.18 = (f32[768]{0:T(1024)}, f32[768]{0:T(1024)S(1)}, u32[]{:S(2)}) copy-start(f32[768]{0:T(1024)S(1)} %get-tuple-element.59) | copy-start | bytes 9220
  177.3 5.0 %copy-start = (bf16[768,768]{1,0:T(8,128)(2,1)S(1)}, bf16[768,768]{1,0:T(8,128)(2,1)}, u32[]{:S(2)}) copy-start(bf16[768,768]{1,0:T(8,128)(2,1)} %get-tuple-element.19) | copy-start | bytes 3538948
  177.3 5.0 %copy-start.9 = (bf16[768,768]{1,0:T(8,128)(2,1)S(1)}, bf16[768,768]{1,0:T(8,128)(2,1)}, u32[]{:S(2)}) copy-start(bf16[768,768]{1,0:T(8,128)(2,1)} %get-tuple-element.20) | copy-start | bytes 3538948
  184.8 60.9 %copy-start.1 = (f32[768,768]{1,0:T(8,128)}, f32[768,768]{1,0:T(8,128)S(1)}, u32[]{:S(2)}) copy-start(f32[768,768]{1,0:T(8,128)S(1)} %get-tuple-element.64) | copy-start | bytes 7077892
  194.5 28.2 %copy-start.26 = (f32[768]{0:T(1024)S(1)}, f32[768]{0:T(1024)}, u32[]{:S(2)}) copy-start(f32[768]{0:T(1024)} %get-tuple-element.57) | copy-start | bytes 9220
  222.8 7.9 %copy-start.34 = (bf16[768,3072]{1,0:T(8,128)(2,1)}, bf16[768,3072]{1,0:T(8,128)(2,1)S(1)}, u32[]{:S(2)}) copy-start(bf16[768,3072]{1,0:T(8,128)(2,1)S(1)} %get-tuple-element.46) | copy-start | bytes 14155780
  231.7 106.3 %collective-permute-start = (bf16[384,768]{1,0:T(8,128)(2,1)}, bf16[384,768]{1,0:T(8,128)(2,1)}, u32[]{:S(2)}, u32[]{:S(2)}) collective-permute-start(bf16[384,768]{1,0:T(8,128)(2,1)} %get-tuple-element.55), channel_id=1, source_target_pairs={{0,2},{1,3},{2,0},{3,1},{4,6},{5,7},{6,4},{7,5},{8,10},{9,11},{10,... | collective-permute-start | bytes 1769480 | tf_op jit(solution)/shard_map/ppermute | solution.py:1102
  233.0 12.7 %copy-start.19 = (f32[768]{0:T(1024)S(1)}, f32[768]{0:T(1024)}, u32[]{:S(2)}) copy-start(f32[768]{0:T(1024)} %copy-done.18) | copy-start | bytes 9220
  233.0 12.7 %copy-start.22 = (f32[768]{0:T(1024)S(1)}, f32[768]{0:T(1024)}, u32[]{:S(2)}) copy-start(f32[768]{0:T(1024)} %fusion.35) | copy-start | bytes 9220
  245.7 9.0 %copy-start.33 = (bf16[768,3072]{1,0:T(8,128)(2,1)}, bf16[768,3072]{1,0:T(8,128)(2,1)S(1)}, u32[]{:S(2)}) copy-start(bf16[768,3072]{1,0:T(8,128)(2,1)S(1)} %get-tuple-element.71) | copy-start | bytes 14155780
  254.7 2.6 copy-start.3
  259.5 4.6 %copy-start.5 = (bf16[768,768]{1,0:T(8,128)(2,1)}, bf16[768,768]{1,0:T(8,128)(2,1)S(1)}, u32[]{:S(2)}) copy-start(bf16[768,768]{1,0:T(8,128)(2,1)S(1)} %get-tuple-element.43) | copy-start | bytes 3538948
  271.1 47.8 %copy-start.20 = (f32[768]{0:T(1024)S(1)}, f32[768]{0:T(1024)}, u32[]{:S(2)}) copy-start(f32[768]{0:T(1024)} %copy-done.18) | copy-start | bytes 9220
  271.1 47.8 %copy-start.23 = (f32[768]{0:T(1024)S(1)}, f32[768]{0:T(1024)}, u32[]{:S(2)}) copy-start(f32[768]{0:T(1024)} %fusion.35) | copy-start | bytes 9220
  271.1 47.8 %copy-start.25 = (f32[768]{0:T(1024)S(1)}, f32[768]{0:T(1024)}, u32[]{:S(2)}) copy-start(f32[768]{0:T(1024)} %get-tuple-element.58) | copy-start | bytes 9220
  316.3 2.5 copy-start.2
  318.8 25.0 %collective-permute-start.2 = (bf16[768,768]{1,0:T(8,128)(2,1)}, bf16[768,768]{1,0:T(8,128)(2,1)}, u32[]{:S(2)}, u32[]{:S(2)}) collective-permute-start(bf16[768,768]{1,0:T(8,128)(2,1)} %slice.78), channel_id=1, source_target_pairs={{0,1},{1,0},{2,3},{3,2},{4,5},{5,4},{6,7},{7,6},{8,9},{9,8},{10,11... | collective-permute-start | bytes 3538952 | tf_op jit(solution)/shard_map/ppermute | solution.py:1171
  335.8 2.3 copy-start.8
  337.3 3.3 copy-start.31
  337.3 9.6 %collective-permute-start.3 = (bf16[768,768]{1,0:T(8,128)(2,1)S(1)}, bf16[768,768]{1,0:T(8,128)(2,1)S(1)}, u32[]{:S(2)}, u32[]{:S(2)}) collective-permute-start(bf16[768,768]{1,0:T(8,128)(2,1)S(1)} %slice.81), channel_id=1, source_target_pairs={{0,1},{1,0},{2,3},{3,2},{4,5},{5,4},{6,7},{7,6},{8,9},{9,8},{10,11... | collective-permute-start | bytes 3538952 | tf_op jit(solution)/shard_map/ppermute | solution.py:1171
  343.8 3.1 copy-start.7
  351.7 102.6 %collective-permute-start.4 = (bf16[384,768]{1,0:T(8,128)(2,1)S(1)}, bf16[384,768]{1,0:T(8,128)(2,1)S(1)}, u32[]{:S(2)}, u32[]{:S(2)}) collective-permute-start(bf16[384,768]{1,0:T(8,128)(2,1)S(1)} %get-tuple-element.51), channel_id=1, source_target_pairs={{0,2},{1,3},{2,0},{3,1},{4,6},{5,7},{6,4},{7,5},{8,10},{9,11},{10,... | collective-permute-start | bytes 1769480 | tf_op jit(solution)/shard_map/ppermute | solution.py:1102
  356.2 5.1 %slice-start = ((s8[4718592]{0:T(1024)(128)(4,1)}), s8[4194304]{0:T(1024)(128)(4,1)S(1)}, s32[]{:S(2)}) async-start(s8[4718592]{0:T(1024)(128)(4,1)} %bitcast.46), calls=%async_computation | async-start | bytes 8388608
  358.4 2.2 copy-start.16
  358.4 2.9 slice-start.1
  358.4 5.5 %slice-start.2 = ((s8[4718592]{0:T(1024)(128)(4,1)}), s8[4194304]{0:T(1024)(128)(4,1)S(1)}, s32[]{:S(2)}) async-start(s8[4718592]{0:T(1024)(128)(4,1)} %bitcast.62), calls=%async_computation.2 | async-start | bytes 8388608
  360.7 3.2 slice-start.3
  361.4 2.5 copy-start.17
  (12 other events, 18.1 us)

commit v3 on v2

--- a/solution.py
+++ b/solution.py
@@ -420,7 +420,7 @@
 class Scatter:
     def __init__(self, at, g_ref, out_ref, buffers, send, recv, local_sem, low, high):
         self.at, self.g, self.out, self.send, self.recv = at, g_ref, out_ref, send, recv
-        self.acc, self.from_pair, self.x1, self.y1, self.x2, self.y2, self.za, self.zb = buffers
+        self.acc, self.stage, self.x1, self.y1, self.x2, self.y2, self.za, self.zb = buffers
         self.local_sem, self.low, self.high = local_sem, low, high
         self.count = (high - low + 1) * CHUNKS
         self.last = at.levels + 2
@@ -441,7 +441,7 @@
         acc = self.acc
         mine = acc.at[index, x, y, rows]
         return {
-            0: (self.g.at[index, :, :, 1 - c, rows], self.from_pair.at[index, :, :, rows], at.pair),
+            0: (self.g.at[index, :, :, 1 - c, rows], acc.at[index, :, :, rows], at.pair),
             1: (acc.at[index, 1 - x, :, rows_a], self.x1.at[item], at.near_x),
             2: (acc.at[index, :, 1 - y, rows_b], self.y1.at[item], at.near_y),
             3: (acc.at[index, x, 1 - y, rows_a], self.y2.at[item], at.near_y),
@@ -469,7 +469,7 @@
     def local(self, item, index, rows):
         return pltpu.make_async_copy(
             self.g.at[index, :, :, self.at.c, rows[0]],
-            self.acc.at[index, :, :, rows[0]],
+            self.stage.at[item % 2],
             self.local_sem.at[item],
         )
 
@@ -491,7 +491,7 @@
             for xs in range(2):
                 for ys in range(2):
                     where = (index, xs, ys, rows[0])
-                    self.add(self.acc, where, self.from_pair[where])
+                    self.add(self.acc, where, self.stage[item % 2, xs, ys])
             self.copy(views, 1, item).start()
             self.copy(views, 2, item).start()
 
@@ -690,7 +690,7 @@
     h = CHUNK // 2
     return [
         pltpu.VMEM((levels, 2, 2, SHARD, D), BF16),
-        pltpu.VMEM((levels, 2, 2, SHARD, D), BF16),
+        pltpu.VMEM((2, 2, 2, CHUNK, D), BF16),
         pltpu.VMEM((items, 2, h, D), BF16),
         pltpu.VMEM((items, 2, CHUNK - h, D), BF16),
         pltpu.VMEM((items, CHUNK - h, D), BF16),
@@ -701,6 +701,53 @@
         pltpu.SemaphoreType.DMA((7, items)),
         pltpu.SemaphoreType.DMA((items,)),
     ]
+
+
+def backward_head(
+    pair,
+    half,
+    q_ref,
+    k_ref,
+    v_ref,
+    bias_ref,
+    g_ref,
+    lt_ref,
+    dt_ref,
+    dq_ref,
+    dk_ref,
+    dv_ref,
+    key_chunk,
+):
+    rows = q_ref.shape[0]
+    keys = k_ref.shape[0]
+    cols = pair_columns(pair)
+    lane = lax.broadcasted_iota(jnp.int32, (key_chunk, LANES), 1)
+    lane_q = lax.broadcasted_iota(jnp.int32, (rows, LANES), 1)
+    own, own_q = lane // HEAD == half, lane_q // HEAD == half
+    spare = lane == (1 - half) * HEAD
+    query_pair = q_ref[:, cols]
+    grad_pair = g_ref[:, cols]
+    query = jnp.where(own_q, query_pair, jnp.ones_like(query_pair))
+    mass = lt_ref[pl.ds(2 * pair + half, 1), :]
+    inner = dt_ref[pl.ds(2 * pair + half, 1), :]
+    zero = jnp.zeros((key_chunk, LANES), BF16)
+    grad_query = jnp.zeros((rows, LANES), F32)
+    for chunk in range(keys // key_chunk):
+        part = pl.ds(chunk * key_chunk, key_chunk)
+        key_pair = k_ref[part, cols]
+        head_key = jnp.where(own, key_pair, jnp.where(spare, bias_ref[part, :], zero))
+        head_value = jnp.where(own, v_ref[part, cols], zero)
+        scores = back_product(head_key, query)
+        soft = jnp.exp(scores - mass)
+        grad_soft = back_product(head_value, grad_pair)
+        grad_scores = (soft * (grad_soft - inner)).astype(BF16)
+        grad_value = matmul(soft.astype(BF16), grad_pair).astype(BF16)
+        grad_key = matmul(grad_scores, query_pair).astype(BF16)
+        grad_query = grad_query + outer_sum(grad_scores, key_pair)
+        dk_ref[part, cols] = jnp.where(own, grad_key, dk_ref[part, cols])
+        dv_ref[part, cols] = jnp.where(own, grad_value, dv_ref[part, cols])
+    merged = (grad_query * HEAD ** (-0.5)).astype(BF16)
+    dq_ref[:, cols] = jnp.where(own_q, merged, dq_ref[:, cols])
 
 
 def vector_row(vec_ref, first, count=D):
@@ -902,43 +949,233 @@
     )(own, vec_part, inputs, bias)
 
 
-def scatter_call_kernel(g_ref, vec_ref, out_ref, vecs_ref, *scratch):
+SCATTER_PARTS = 11
+
+
+def backward_call_kernel(
+    q_ref,
+    k_ref,
+    v_ref,
+    bias_ref,
+    g_ref,
+    lt_ref,
+    dt_ref,
+    n_ref,
+    x_ref,
+    gm_ref,
+    vecs_ref,
+    vec_grad_ref,
+    w0_ref,
+    rest_ref,
+    result_ref,
+    outputs_ref,
+    grad_in_ref,
+    out_ref,
+    vec_out_ref,
+    dq_ref,
+    dk_ref,
+    dv_ref,
+    rk_ref,
+    rv_ref,
+    gi_ref,
+    g0_ref,
+    pair_send,
+    pair_recv,
+    misc_send,
+    misc_recv,
+    misc_local,
+    *scratch,
+):
     at = Place()
-    sums, came, vec_send, vec_recv = scratch[11:]
-    sums[0] = vec_ref[...]
+    rows = x_ref.shape[0]
+    slots = rows // 2
+    mine, other = pl.ds(0, rows), pl.ds(rows, rows)
+    kept, sent = pl.ds(0, slots), pl.ds(slots, slots)
+    rest_scratch, scratch = scratch[:SCATTER_PARTS], scratch[SCATTER_PARTS:]
+    base_scratch, scratch = scratch[:SCATTER_PARTS], scratch[SCATTER_PARTS:]
+    sums, came, vec_send, vec_recv = scratch
+    rest = Scatter(
+        at, rest_ref, out_ref, rest_scratch[:8], *rest_scratch[8:], 1, at.levels - 1
+    )
+    base = Scatter(at, g0_ref, out_ref, base_scratch[:8], *base_scratch[8:], 0, 0)
+    total = Total(at, sums, came, vec_send, vec_recv)
+    out_kept = pltpu.make_async_copy(
+        result_ref.at[kept], outputs_ref.at[at.y], misc_local.at[0]
+    )
+    out_kept.start()
     at.barrier()
-    total = Total(at, sums, came, vec_send, vec_recv)
-    scatter = Scatter(
-        at, g_ref, out_ref, scratch[:8], scratch[8], scratch[9], scratch[10], 0, at.levels - 1
-    )
-
-    def step(number, carry):
-        scatter.step(number)
-        total.step(number)
+    out_swap = remote(
+        result_ref.at[sent], outputs_ref.at[at.y], misc_send.at[0], misc_recv.at[0], at.near_y
+    )
+
+    def exchange(kind, pair):
+        source = (dk_ref, dv_ref)[kind]
+        target = (rk_ref, rv_ref)[kind]
+        return remote(
+            source.at[other, pair_columns(pair)],
+            target.at[:, pair_columns(pair)],
+            pair_send.at[kind, pair],
+            pair_recv.at[kind, pair],
+            at.pair,
+        )
+
+    def head_step(head, carry):
+        pair, half = head // 2, head % 2
+        rest.step(head)
+        backward_head(
+            pair,
+            half,
+            q_ref,
+            k_ref,
+            v_ref,
+            bias_ref,
+            g_ref,
+            lt_ref,
+            dt_ref,
+            dq_ref,
+            dk_ref,
+            dv_ref,
+            ROW_CHUNK,
+        )
+
+        @pl.when(half == 1)
+        def _():
+            exchange(0, pair).start()
+            exchange(1, pair).start()
+
         return carry
 
-    lax.fori_loop(0, scatter.steps, step, 0)
-    total.finish(vecs_ref)
-    scatter.finish()
-
-
-def scatter_call(grads, vec_part, levels):
+    lax.fori_loop(0, HEADS, head_step, 0)
+    out_swap.start()
+    rest.step(HEADS)
+
+    def gather_pair(pair, carry):
+        for kind in range(2):
+            exchange(kind, pair).wait_recv()
+        return carry
+
+    lax.fori_loop(0, PAIRS, gather_pair, 0)
+    for chunk in range(rows // ROW_CHUNK):
+        part = pl.ds(chunk * ROW_CHUNK, ROW_CHUNK)
+        dk_ref[part, :] = (dk_ref[part, :].astype(F32) + rk_ref[part, :].astype(F32)).astype(BF16)
+        dv_ref[part, :] = (dv_ref[part, :].astype(F32) + rv_ref[part, :].astype(F32)).astype(BF16)
+    grads = (dq_ref, dk_ref, dv_ref)
+    for which in range(3):
+        grad = grads[which][mine, :]
+        for block in range(2):
+            size = D // 2
+            piece = outer_sum(n_ref[:, block * size : (block + 1) * size], grad).astype(BF16)
+            for unit in range(size // CHUNK):
+                number = (which * D + block * size) // CHUNK + unit
+                shard = number // CHUNKS
+                first = number % CHUNKS * CHUNK
+                g0_ref[0, shard // 4, shard // 2 % 2, shard % 2, first : first + CHUNK, :] = piece[
+                    unit * CHUNK : (unit + 1) * CHUNK
+                ]
+        if which < 2:
+            rest.step(HEADS + 1 + which)
+    base.step(0)
+    for number in range(HEADS + 3, rest.steps):
+        rest.step(number)
+    base.step(1)
+    sums[0] = vec_grad_ref[...]
+    gain = vector_row(vecs_ref, 0)
+    weights = [rows_of(w0_ref, which * D, D) for which in range(3)]
+    column = [jnp.zeros((1, D), F32) for _ in range(4)]
+    for chunk in range(rows // ROW_CHUNK):
+        part = pl.ds(chunk * ROW_CHUNK, ROW_CHUNK)
+        grad_normed = sum(back_product(grads[which][part, :], weights[which]) for which in range(3))
+        frames = x_ref[part, :].astype(F32)
+        centered = frames - jnp.mean(frames, axis=-1, keepdims=True)
+        spread = lax.rsqrt(jnp.mean(centered * centered, axis=-1, keepdims=True) + 1e-05)
+        unit_rows = centered * spread
+        scaled = grad_normed * gain
+        inner = jnp.mean(scaled * unit_rows, axis=-1, keepdims=True)
+        shifted = scaled - jnp.mean(scaled, axis=-1, keepdims=True) - unit_rows * inner
+        gi_ref[part, :] = (gm_ref[part, :] + spread * shifted).astype(BF16)
+        parts = (
+            grad_normed * unit_rows,
+            grad_normed,
+            dq_ref[part, :].astype(F32),
+            dv_ref[part, :].astype(F32),
+        )
+        for i in range(4):
+            column[i] = column[i] + jnp.sum(parts[i], axis=0, keepdims=True)
+        base.step(2 + chunk)
+    for i in range(4):
+        for j in range(D // 128):
+            sums[0, i * (D // 128) + j : i * (D // 128) + j + 1, :] = column[i][
+                :, j * 128 : (j + 1) * 128
+            ]
+    total.step(0)
+    in_kept = pltpu.make_async_copy(gi_ref.at[kept], grad_in_ref.at[at.y], misc_local.at[1])
+    in_swap = remote(
+        gi_ref.at[sent], grad_in_ref.at[at.y], misc_send.at[1], misc_recv.at[1], at.near_y
+    )
+    in_kept.start()
+    in_swap.start()
+    total.step(1)
+
+    def last(number, carry):
+        base.step(number)
+        total.step(number - 3)
+        return carry
+
+    lax.fori_loop(2 + rows // ROW_CHUNK, total.steps + 3, last, 0)
+    total.finish(vec_out_ref)
+    base.finish()
+    rest.finish()
+    for swap in (out_swap, in_swap):
+        swap.wait_send()
+        swap.wait_recv()
+    out_kept.wait()
+    in_kept.wait()
+
+    def sent_pair(pair, carry):
+        for kind in range(2):
+            exchange(kind, pair).wait_send()
+        return carry
+
+    lax.fori_loop(0, PAIRS, sent_pair, 0)
+
+
+def backward_call(operands, rest, result, shape, levels):
+    rows = shape[0] * shape[1]
+    vec_rows = operands[11].shape[0]
     vmem = pl.BlockSpec(memory_space=pltpu.VMEM)
     anywhere = pl.BlockSpec(memory_space=pl.ANY)
     return pl.pallas_call(
-        scatter_call_kernel,
+        backward_call_kernel,
         out_shape=(
+            jax.ShapeDtypeStruct(shape, BF16),
+            jax.ShapeDtypeStruct(shape, BF16),
             jax.ShapeDtypeStruct((SHARD, D), F32),
-            jax.ShapeDtypeStruct(vec_part.shape, F32),
+            jax.ShapeDtypeStruct((vec_rows, 128), F32),
         ),
-        in_specs=[anywhere, vmem],
-        out_specs=(vmem, vmem),
-        scratch_shapes=scatter_scratch(levels) + total_scratch(vec_part.shape[0]),
+        in_specs=[vmem] * 13 + [anywhere] * 2,
+        out_specs=(anywhere, anywhere, vmem, vmem),
+        scratch_shapes=[
+            pltpu.VMEM((rows, D), BF16),
+            pltpu.VMEM((2 * rows, D), BF16),
+            pltpu.VMEM((2 * rows, D), BF16),
+            pltpu.VMEM((rows, D), BF16),
+            pltpu.VMEM((rows, D), BF16),
+            pltpu.VMEM((rows, D), BF16),
+            pltpu.VMEM((1, 2, 2, 2, SHARD, D), BF16),
+            pltpu.SemaphoreType.DMA((2, PAIRS)),
+            pltpu.SemaphoreType.DMA((2, PAIRS)),
+            pltpu.SemaphoreType.DMA((2,)),
+            pltpu.SemaphoreType.DMA((2,)),
+            pltpu.SemaphoreType.DMA((2,)),
+        ]
+        + scatter_scratch(levels - 1)
+        + scatter_scratch(1)
+        + total_scratch(vec_rows),
         compiler_params=pltpu.CompilerParams(
             collective_id=1, has_side_effects=True, vmem_limit_bytes=VMEM_LIMIT
         ),
-        name="scatter_sum",
-    )(grads, vec_part)
+        name="attend_scatter",
+    )(*operands, rest, result)
 
 
 def plain_local(inputs, lengths, matrices, vectors, cotangent):
@@ -1089,7 +1326,6 @@
     devices = lax.axis_size("seq") * lax.axis_size("tok")
     rows = seq_count * local_slots
     across = [(i, (i + 2) % 4) for i in range(4)]
-    partner = [(i, i + 1 - 2 * (i % 2)) for i in range(4)]
 
     def pick(array, index):
         return lax.dynamic_index_in_dim(array, index, 0, keepdims=False)
@@ -1097,17 +1333,12 @@
     def to_sequence(array):
         other = lax.ppermute(pick(array, 1 - half), "tok", across)
         return jnp.concatenate([pick(array, half), other], axis=0)
-
-    def from_sequence(array):
-        other = lax.ppermute(array[local_slots:], "tok", across)
-        kept = array[:local_slots]
-        return jnp.where(half == 0, jnp.stack([kept, other]), jnp.stack([other, kept]))
 
     own = matrices.reshape(SHARD, width).astype(BF16)
     vec_count = vectors.shape[0]
     vec_total = vec_count * devices
     vec_part = lax.dynamic_update_slice(
-        jnp.zeros((vec_total,), F32), vectors.astype(BF16).astype(F32), (place * vec_count,)
+        jnp.zeros((vec_total,), F32), lax.reduce_precision(vectors, 8, 7), (place * vec_count,)
     ).reshape(vec_total // 128, 128)
     length = pick(lengths, half)
     slot = jnp.arange(local_slots, dtype=jnp.int32)
@@ -1131,8 +1362,6 @@
         bias_up,
         bias_down,
     ) = split_vectors(vecs.reshape(-1))
-    first_rows = w_first.reshape(-1, width)
-    w_query, w_key, w_value = (first_rows[i * D : (i + 1) * D] for i in range(3))
     rest_rows = w_rest.reshape(-1, width)
     w_out = rest_rows[:D]
     w_up = rest_rows[D : D + FF].reshape(D, FF)
@@ -1143,7 +1372,6 @@
     hidden = matmul(normed_two, w_up) + bias_up
     active = jax.nn.gelu(hidden, approximate=False).astype(BF16)
     result = middle + (matmul(active, w_down) + bias_down)
-    outputs = from_sequence(result.astype(BF16))
 
     grad_out_wide = grad_out.astype(F32)
     d_down = outer_sum(active, grad_out)
@@ -1163,51 +1391,33 @@
     grad_attended = back_product(grad_branch, w_out).astype(BF16)
     inner = (grad_attended.astype(F32) * attended.astype(F32)).reshape(rows, HEADS, HEAD).sum(-1)
     inner = jnp.pad(inner.T, ((0, 16 - HEADS), (0, 0)))
-    grad_query, grad_keys, grad_values = attend_back(
-        scaled, keys, values, bias, grad_attended, lt, inner
-    )
-
-    def pair_sum(array):
-        other = lax.ppermute(array[rows:], "tok", partner)
-        return (array[:rows].astype(F32) + other.astype(F32)).astype(BF16)
-
-    grad_key = pair_sum(grad_keys)
-    grad_value = pair_sum(grad_values)
-    d_query = outer_sum(normed, grad_query)
-    d_key = outer_sum(normed, grad_key)
-    d_value = outer_sum(normed, grad_value)
-    d_bias_query = column_sum(grad_query)
-    d_bias_value = column_sum(grad_value)
-    grad_normed = (
-        back_product(grad_query, w_query)
-        + back_product(grad_key, w_key)
-        + back_product(grad_value, w_value)
-    )
-    first_value, leading_pullback = jax.vjp(layer_norm, token_rows, gain_one, first_norm_shift)
-    grad_rows_norm, d_gain_one, d_shift_one = leading_pullback(grad_normed)
-    grad_inputs = from_sequence((grad_middle + grad_rows_norm).astype(BF16))
-    matrix_rows = jnp.concatenate(
-        [
-            piece.astype(BF16).reshape(-1, width)
-            for piece in (d_query, d_key, d_value, d_out, d_up, d_down)
-        ]
-    )
-    flat_vector_grads = jnp.concatenate(
-        [
-            d_gain_one,
-            d_shift_one,
-            d_bias_query,
-            d_bias_value,
-            d_bias_out,
-            d_gain_two,
-            d_shift_two,
-            d_bias_up,
-            down_bias_gradient,
-        ]
-    )
-    grad_rows, grad_vecs = scatter_call(
-        matrix_rows.reshape(levels, 2, 2, 2, SHARD, width),
-        flat_vector_grads.reshape(vec_part.shape),
+    nothing = jnp.zeros((D,), F32)
+    vec_grads = jnp.concatenate(
+        [nothing] * 4
+        + [d_bias_out, d_gain_two, d_shift_two, d_bias_up, down_bias_gradient]
+    ).reshape(vec_part.shape)
+    rest_grads = jnp.concatenate(
+        [piece.astype(BF16).reshape(-1, width) for piece in (d_out, d_up, d_down)]
+    ).reshape(levels - 1, 2, 2, 2, SHARD, width)
+    outputs, grad_inputs, grad_rows, grad_vecs = backward_call(
+        (
+            scaled,
+            keys,
+            values,
+            bias,
+            grad_attended,
+            lt,
+            inner,
+            normed,
+            frames,
+            grad_middle,
+            vecs,
+            vec_grads,
+            w_first,
+        ),
+        rest_grads,
+        result.astype(BF16),
+        inputs.shape,
         levels,
     )
     grad_matrices = grad_rows.reshape(-1)

time: 460 us -> 441 us (0.959)
  the two profiles are of different devices: /device:TPU:24 before, /device:TPU:0 now
where the time goes in v3:
time: 441 us; the launch traced here: 438 us
  Pallas kernels  281 us (64%)
  matrix products  77.1 us (17%)
  local copies, waits for them, and re-layouts  48.7 us (11%)
  other arithmetic  26.8 us (6%)
    pallas_call x1, Pallas kernels, forward_call(): pl.pallas_call(forward_call_kernel, out_shape=(low(rows, D), low(rows, D)...  161 us
    pallas_call x1, Pallas kernels, backward_call(): pl.pallas_call(backward_call_kernel, out_shape=(jax.ShapeDtypeStruct(shap...  120 us
    dot_general x3, matrix products, matmul(): return jnp.dot(left_operand, right_operand, preferred_element_type=F32)  39.1 us
    dot_general x3, matrix products, back_product(): lax.dot_general(gradient, weight, (((1,), (1,)), ((), ())), preferred_ele...  22.6 us
    concatenate x1, other arithmetic, fast_local(): jnp.concatenate([piece.astype(BF16).reshape(-1, width) for piece in (d_ou...  21.5 us
    dot_general x3, matrix products, outer_sum(): lax.dot_general(left_operand, right_operand, (((0,), (0,)), ((), ())), pr...  15.5 us
    unnamed x41, local copies, waits for them, and re-layouts  10 us
  transfers between devices with their start and end apart: 1, of which 0 were waited for; matrix products, arithmetic and copies ran while one was open for 14% of the time, Pallas kernels for 37%

profile of v3, /device:TPU:0, one launch (start us, length us, event | category | flops | bytes accessed | tf_op | source)
XLA Modules:
  0.0 437.6 jit_solution(14356211496437681808)
XLA Ops:
  0.7 2.1 dynamic-slice_bitcast_fusion.1
  2.8 3.0 collective-permute-start
  5.8 1.2 convert_element_type.60
  7.0 1.2 convert_element_type.61.own_ref
  8.1 1.2 dynamic_slice.14
  11.9 161.4 %gather_attend.1 = (bf16[768,768]{1,0:T(8,128)(2,1)}, bf16[768,768]{1,0:T(8,128)(2,1)}, bf16[768,768]{1,0:T(8,128)(2,1)}, bf16[1536,768]{1,0:T(8,128)(2,1)}, bf1...) custom-call(bf16[288,768]{1,0:T(8,128)(2,1)} %convert_element_type.6, ...), custom_call_target="tpu_custom_call" | custom-call | tf_op jit(solution)/shard_map/gather_attend/pallas_call | solution.py:918
  173.3 1.4 slice_bitcast_fusion.1
  174.6 1.3 slice_bitcast_fusion
  176.0 5.0 %slice.38 = bf16[3072,768]{1,0:T(8,128)(2,1)} slice(bf16[6912,768]{1,0:T(8,128)(2,1)} %bitcast.34), slice={[768:3840], [0:768]} | slice | bytes 9437184 | tf_op jit(solution)/shard_map/slice | solution.py:1367
  181.0 2.5 fusion.22
  183.9 8.5 %reshape.112 = bf16[768,3072]{1,0:T(8,128)(2,1)} reshape(bf16[3072,768]{1,0:T(8,128)(2,1)} %slice.38) | data formatting | bytes 9437184 | tf_op jit(solution)/shard_map/reshape | solution.py:1367
  192.4 27.7 %multiply_convert_fusion = (bf16[768,3072]{1,0:T(8,128)(2,1)S(1)}, f32[768,3072]{1,0:T(8,128)}, f32[768,3072]{1,0:T(8,128)}) fusion(f32[3072]{0:T(1024)} %slice_bitcast_fusion, bf16[768,3072]{1,0:T(8,128)(2,1)} %reshape.112, f32[768,768]{1,0:T(8,128)S(1)} %get-tuple-element.49, f32[768]{0:T(1024)} %get-tuple-element.45, f32[768]{0:T(1024)S(1)} %get-tuple-element.46, ...), kind=kOutput, calls=%fused_computation.3 | convolution fusion | flops 3782541312 | bytes 30695424 | tf_op jit(solution)/shard_map/dot_general | solution.py:29
  220.1 8.9 %add_convert_fusion.1.result_ref = bf16[768,768]{1,0:T(8,128)(2,1)} fusion(f32[768,768]{1,0:T(8,128)S(1)} %get-tuple-element.49, bf16[768,3072]{1,0:T(8,128)(2,1)S(1)} %get-tuple-element.35, bf16[6912,768]{1,0:T(8,128)(2,1)} %bitcast.36, f32[768]{0:T(1024)S(1)} %copy-done.13), kind=kOutput, calls=%fused_computation.28 | convolution fusion | flops 3625648128 | bytes 12979200 | tf_op jit(solution)/shard_map/dot_general | solution.py:29
  229.6 13.5 %convert_reduce_fusion = (f32[3072]{0:T(1024)}, bf16[768,3072]{1,0:T(8,128)(2,1)S(1)}) fusion(f32[768,3072]{1,0:T(8,128)} %get-tuple-element.36, bf16[6912,768]{1,0:T(8,128)(2,1)} %bitcast.37, bf16[384,768]{1,0:T(8,128)(2,1)S(1)} %collective-permute-done, bf16[384,768]{1,0:T(8,128)(2,1)S(1)} %get-tuple-element.42, f32[768,3072]{1,0:T(8,128)} %get-tuple-element.50, ...), kind=kOutput, calls=%fused_computation.4 | convolution fusion | flops 3666342912 | bytes 29515776 | tf_op jit(solution)/shard_map/dot_general | solution.py:39
  243.1 4.8 %multiply_reduce_fusion = (f32[768]{0:T(1024)}, f32[768]{0:T(1024)S(1)}, f32[768]{0:T(1024)}, f32[768,768]{1,0:T(8,128)S(1)}) fusion(f32[768,768]{1,0:T(8,128)S(1)} %get-tuple-element.49, f32[768]{0:T(1024)S(1)} %fusion.16, f32[768]{0:T(1024)S(1)} %broadcast_multiply_fusion, f32[768]{0:T(1024)S(1)} %get-tuple-element.46, ...), kind=kOutput, calls=%fused_computation.29 | convolution fusion | flops 3628594944 | bytes 14174208 | tf_op jit(solution)/shard_map/dot_general | solution.py:39
  247.9 6.5 %convolution_convert_fusion.1 = bf16[768,3072]{1,0:T(8,128)(2,1)} fusion(bf16[768,3072]{1,0:T(8,128)(2,1)S(1)} %get-tuple-element.55, f32[768,768]{1,0:T(8,128)S(1)} %get-tuple-element.49, f32[768]{0:T(1024)S(1)} %copy-done.12, f32[768]{0:T(1024)S(1)} %get-tuple-element.46, f32[768]{0:T(1024)S(1)} %fusion.16, f32[768]{0:T(1024)S(1)} %broadcast_multiply_fusion), kind=kOutput, calls=%fused_computation.20 | convolution fusion | flops 3629187072 | bytes 11808768 | tf_op jit(solution)/shard_map/dot_general | solution.py:33
  256.6 4.3 convert_multiply_fusion
  260.8 2.1 convolution_convert_fusion.2
  263.0 2.2 copy.13
  266.0 1.4 pad.4.dt_ref
  267.4 8.5 %reshape.115 = bf16[3072,768]{1,0:T(8,128)(2,1)} reshape(bf16[768,3072]{1,0:T(8,128)(2,1)} %convolution_convert_fusion.1) | data formatting | bytes 9437184 | tf_op jit(solution)/shard_map/reshape | solution.py:1400
  275.9 1.3 constant_dynamic-update-slice_fusion.4
  277.2 1.3 constant_dynamic-update-slice_fusion.3
  278.5 1.3 constant_dynamic-update-slice_fusion.2
  279.8 1.3 constant_dynamic-update-slice_fusion.1
  281.1 1.3 constant_dynamic-update-slice_fusion
  282.4 6.9 %convolution_convert_fusion = bf16[3072,768]{1,0:T(8,128)(2,1)S(1)} fusion(bf16[768,3072]{1,0:T(8,128)(2,1)} %copy-done.14, bf16[384,768]{1,0:T(8,128)(2,1)S(1)} %collective-permute-done, bf16[384,768]{1,0:T(8,128)(2,1)S(1)} %get-tuple-element.42), kind=kOutput, calls=%fused_computation.19 | convolution fusion | flops 3628597248 | bytes 10616832 | tf_op jit(solution)/shard_map/dot_general | solution.py:33
  289.3 21.5 %pad_maximum_fusion = bf16[6912,768]{1,0:T(8,128)(2,1)} fusion(bf16[3072,768]{1,0:T(8,128)(2,1)S(1)} %convolution_convert_fusion, bf16[3072,768]{1,0:T(8,128)(2,1)S(1)} %copy-done.1, bf16[768,768]{1,0:T(8,128)(2,1)S(1)} %copy-done.6), kind=kLoop, calls=%fused_computation.1 | loop fusion | flops 31850496 | bytes 21233664 | tf_op jit(solution)/shard_map/concatenate | solution.py:1399
  310.8 119.6 %attend_scatter.1 = (bf16[2,384,768]{2,1,0:T(8,128)(2,1)}, bf16[2,384,768]{2,1,0:T(8,128)(2,1)}, f32[288,768]{1,0:T(8,128)}, f32[72,128]{1,0:T(8,128)}) custom-call(bf16[768,768]{1,0:T(8,128)(2,1)} %get-tuple-element.18.q_ref, bf16[1536,768]{1,0:T(8,128)(2,1)} %get-tuple-element.19.k_ref, bf16[1536,768]{1,0:T(8,128)(2,1)} %get-tuple-element.20.v_ref, ...), custom_call_target="tpu_custom_call" | custom-call | tf_op jit(solution)/shard_map/attend_scatter/pallas_call | solution.py:1147
  430.4 2.2 reshape.117
  432.7 1.3 dynamic_slice.17
  434.0 2.4 copy.24
  (52 shorter events, 7.5 us)
Async XLA Ops:
  2.8 226.8 %collective-permute-start = (bf16[384,768]{1,0:T(8,128)(2,1)}, bf16[384,768]{1,0:T(8,128)(2,1)S(1)}, u32[]{:S(2)}, u32[]{:S(2)}) collective-permute-start(bf16[384,768]{1,0:T(8,128)(2,1)} %get-tuple-element.43), channel_id=1, source_target_pairs={{0,2},{1,3},{2,0},{3,1},{4,6},{5,7},{6,4},{7,5},{8,10},{9,11},{10,... | collective-permute-start | bytes 1769480 | tf_op jit(solution)/shard_map/ppermute | solution.py:1334
  10.2 1.7 copy-start.7
  176.0 5.0 %copy-start.2 = (bf16[768,768]{1,0:T(8,128)(2,1)S(1)}, bf16[768,768]{1,0:T(8,128)(2,1)}, u32[]{:S(2)}) copy-start(bf16[768,768]{1,0:T(8,128)(2,1)} %get-tuple-element.21.x_ref) | copy-start | bytes 3538948
  176.0 5.0 %copy-start.4 = (bf16[768,768]{1,0:T(8,128)(2,1)S(1)}, bf16[768,768]{1,0:T(8,128)(2,1)}, u32[]{:S(2)}) copy-start(bf16[768,768]{1,0:T(8,128)(2,1)} %get-tuple-element.22) | copy-start | bytes 3538948
  192.4 27.7 %copy-start.13 = (f32[768]{0:T(1024)S(1)}, f32[768]{0:T(1024)}, u32[]{:S(2)}) copy-start(f32[768]{0:T(1024)} %get-tuple-element.44) | copy-start | bytes 9220
  220.0 8.9 %copy-start.14 = (bf16[768,3072]{1,0:T(8,128)(2,1)}, bf16[768,3072]{1,0:T(8,128)(2,1)S(1)}, u32[]{:S(2)}) copy-start(bf16[768,3072]{1,0:T(8,128)(2,1)S(1)} %get-tuple-element.35) | copy-start | bytes 14155780
  220.0 9.5 %copy-start.9 = (f32[3072]{0:T(1024)S(1)}, f32[3072]{0:T(1024)}, u32[]{:S(2)}) copy-start(f32[3072]{0:T(1024)} %slice_bitcast_fusion) | copy-start | bytes 36868
  220.1 23.1 %slice-start = ((s8[4718592]{0:T(1024)(128)(4,1)}), s8[4194304]{0:T(1024)(128)(4,1)S(1)}, s32[]{:S(2)}) async-start(s8[4718592]{0:T(1024)(128)(4,1)} %bitcast.32), calls=%async_computation | async-start | bytes 8388608
  229.6 13.5 %slice-start.1 = ((s8[4718592]{0:T(1024)(128)(4,1)}), s8[524288]{0:T(1024)(128)(4,1)S(1)}, s32[]{:S(2)}) async-start(s8[4718592]{0:T(1024)(128)(4,1)} %bitcast.32), calls=%async_computation.1 | async-start | bytes 1048576
  243.1 4.8 %copy-start.12 = (f32[768]{0:T(1024)S(1)}, f32[768]{0:T(1024)}, u32[]{:S(2)}) copy-start(f32[768]{0:T(1024)} %get-tuple-element.45) | copy-start | bytes 9220
  255.3 1.3 copy-start.5
  255.8 7.2 %copy-start = (f32[768,768]{1,0:T(8,128)}, f32[768,768]{1,0:T(8,128)S(1)}, u32[]{:S(2)}) copy-start(f32[768,768]{1,0:T(8,128)S(1)} %get-tuple-element.38.gm_ref) | copy-start | bytes 7077892
  267.4 9.8 %copy-start.11 = (f32[768]{0:T(1024)S(1)}, f32[768]{0:T(1024)}, u32[]{:S(2)}) copy-start(f32[768]{0:T(1024)} %get-tuple-element.32) | copy-start | bytes 9220
  267.4 11.1 %copy-start.10 = (f32[768]{0:T(1024)S(1)}, f32[768]{0:T(1024)}, u32[]{:S(2)}) copy-start(f32[768]{0:T(1024)} %get-tuple-element.34) | copy-start | bytes 9220
  267.4 12.4 %copy-start.8 = (f32[3072]{0:T(1024)S(1)}, f32[3072]{0:T(1024)}, u32[]{:S(2)}) copy-start(f32[3072]{0:T(1024)} %get-tuple-element.54) | copy-start | bytes 36868
  282.4 6.9 %copy-start.1 = (bf16[3072,768]{1,0:T(8,128)(2,1)S(1)}, bf16[3072,768]{1,0:T(8,128)(2,1)}, u32[]{:S(2)}) copy-start(bf16[3072,768]{1,0:T(8,128)(2,1)} %reshape.115) | copy-start | bytes 14155780
  282.4 6.9 %copy-start.6 = (bf16[768,768]{1,0:T(8,128)(2,1)S(1)}, bf16[768,768]{1,0:T(8,128)(2,1)}, u32[]{:S(2)}) copy-start(bf16[768,768]{1,0:T(8,128)(2,1)} %convolution_convert_fusion.2) | copy-start | bytes 3538948
  430.4 6.0 %copy-start.3 = (bf16[2,384,768]{2,1,0:T(8,128)(2,1)S(1)}, bf16[2,384,768]{2,1,0:T(8,128)(2,1)}, u32[]{:S(2)}) copy-start(bf16[2,384,768]{2,1,0:T(8,128)(2,1)} %get-tuple-element.65) | copy-start | bytes 3538948
